TPU v7x, 512 devices: a whole 4x8x8 slice. The times are simulated.
512 devices in a mesh: seq: 64 (over y_lo, z, x), head: 8 (over y_hi, core).
Axes of the slice: x: 4, y: 8 (y_hi: 4, y_lo: 2; y = y_hi * 2 + y_lo), z: 8, core: 2. Of those that a mesh axis runs over, the one named last changes fastest.
Arguments:
- values: bfloat16 [2, 4096, 4096], P(None, 'seq', 'head'), may hold values from -6 to 6
- keys_b: bfloat16 [2, 4096, 128], P(None, 'seq'), may hold values from -0.29882812 to 0.29882812
- queries_c: bfloat16 [2, 4096, 128], P(None, 'seq'), may hold values from -0.29882812 to 0.29882812
- forget: float32 [2, 64, 4096], P(None, 'head', 'seq'), may hold values from 0 to 2
- skip: float32 [64], P('head'), may hold values from 0.5 to 1.5
- cotangent: bfloat16 [2, 4096, 4096], P(None, 'seq', 'head'), may hold values from -0.59765625 to 0.59765625
Outputs:
- mixed: bfloat16 [2, 4096, 4096], P(None, 'seq', 'head')
- grad_values: bfloat16 [2, 4096, 4096], P(None, 'seq', 'head')
- grad_bc: float32 [2, 2, 4096, 128], P(None, None, ('seq', 'head'))
All inputs are finite; a program needn't handle non-finite values.
Results may differ from a plain program's by a relative error of at most 0.012.
Values sent between devices are 32-bit elements; how exact they have to be, the bound alone decides.
A program may use at most 128 MiB of HBM per device.

v0:
```python
import jax
import jax.numpy as jnp
from jax import lax
from jax.sharding import PartitionSpec as P


def shifted(block, axis, distance):
    devices = range(lax.axis_size(axis))
    route = [(i - distance, i) for i in devices if i - distance in devices]
    return lax.ppermute(block, axis, route)


def own_state(values, keys_wide, logcum):
    seq_count, rows, wide = values.shape
    head_count = logcum.shape[1]
    tail_decay = jnp.exp(logcum[..., -1:] - logcum)
    scaled = values.astype(jnp.float32).reshape(seq_count, rows, head_count, wide // head_count)
    scaled = scaled * jnp.transpose(tail_decay, (0, 2, 1))[..., None]
    return jnp.einsum("suhp,sun->shpn", scaled, keys_wide, preferred_element_type=jnp.float32)


def read_state(queries_wide, logcum, carried):
    inner_part = jnp.einsum(
        "stn,shpn->sthp", queries_wide, carried, preferred_element_type=jnp.float32
    )
    return inner_part * jnp.transpose(jnp.exp(logcum), (0, 2, 1))[..., None]


def block_pass(values, keys_wide, queries_wide, scores, forget, skip, carried):
    seq_count, rows, wide = values.shape
    head_count = skip.shape[0]
    head_width = wide // head_count
    logcum = jnp.cumsum(-forget, axis=-1)
    causal = jnp.arange(rows)[:, None] >= jnp.arange(rows)[None, :]
    log_gap = logcum[..., :, None] - logcum[..., None, :]
    decay_mask = jnp.where(causal, jnp.exp(jnp.where(causal, log_gap, 0.0)), 0.0)
    weights = (scores[:, None] * decay_mask).astype(jnp.bfloat16)
    by_head = values.reshape(seq_count, rows, head_count, head_width)
    own_part = jnp.einsum("shtu,suhp->sthp", weights, by_head, preferred_element_type=jnp.float32)
    summed = (
        own_part
        + read_state(queries_wide, logcum, carried)
        + skip[:, None] * by_head.astype(jnp.float32)
    )
    mixed = summed.reshape(seq_count, rows, wide).astype(jnp.bfloat16)
    final_state = jnp.exp(logcum[..., -1])[..., None, None] * carried + own_state(
        values, keys_wide, logcum
    )
    return (mixed, final_state)


def shards(values, keys_b, queries_c, forget, skip, cotangent):
    seq_count, rows, wide = values.shape
    head_count = skip.shape[0]
    head_width = wide // head_count
    state_size = keys_b.shape[-1]
    keys_wide = keys_b.astype(jnp.float32)
    queries_wide = queries_c.astype(jnp.float32)
    scores = jnp.einsum("stn,sun->stu", queries_c, keys_b, preferred_element_type=jnp.float32)
    logcum = jnp.cumsum(-forget, axis=-1)
    carry_decay = jnp.exp(logcum[..., -1])
    state_local = own_state(values, keys_wide, logcum)
    blank = jnp.zeros((seq_count, head_count, head_width, state_size), jnp.float32)
    hops = lax.axis_size("seq") - 1
    decay_wide = carry_decay[..., None, None]
    _, read_pull = jax.vjp(lambda state: read_state(queries_wide, logcum, state), blank)
    incoming = cotangent.astype(jnp.float32).reshape(seq_count, rows, head_count, head_width)
    seed = read_pull(incoming)[0]

    def hop_forward(step, current):
        return shifted(decay_wide * current + state_local, "seq", 1)

    def hop_backward(step, current):
        return shifted(decay_wide * current + seed, "seq", -1)

    carried = lax.fori_loop(0, hops, hop_forward, blank)
    returned = lax.fori_loop(0, hops, hop_backward, blank)

    def whole(value_part, key_part, query_part, score_part, forget_part):
        return block_pass(value_part, key_part, query_part, score_part, forget_part, skip, carried)

    outputs, pullback = jax.vjp(whole, values, keys_wide, queries_wide, scores, forget)
    grads = pullback((cotangent, returned))
    score_grad = grads[3]
    grad_query = grads[2] + jnp.einsum(
        "stu,sun->stn", score_grad, keys_wide, preferred_element_type=jnp.float32
    )
    grad_key = grads[1] + jnp.einsum(
        "stu,stn->sun", score_grad, queries_wide, preferred_element_type=jnp.float32
    )
    grad_bc = lax.psum_scatter(
        jnp.stack([grad_key, grad_query]), "head", scatter_dimension=2, tiled=True
    )
    return (outputs[0], grads[0], grad_bc)


def solution(mesh):
    in_specs = (
        P(None, "seq", "head"),
        P(None, "seq", None),
        P(None, "seq", None),
        P(None, "head", "seq"),
        P("head"),
        P(None, "seq", "head"),
    )
    out_specs = (
        P(None, "seq", "head"),
        P(None, "seq", "head"),
        P(None, None, ("seq", "head"), None),
    )
    return jax.shard_map(shards, mesh=mesh, in_specs=in_specs, out_specs=out_specs, check_vma=False)
```

profile of v0, /device:TPU:1, one launch (start us, length us, event | category | flops | bytes accessed | tf_op | source)
XLA Modules:
  0.0 2263.9 jit_solution(13475841691747630256)
XLA Ops:
  11.0 945.7 %while.21 = (s32[]{:T(128)}, f32[2,8,64,128]{3,2,1,0:T(8,128)S(1)}, f32[2,8,1,1]{1,0,3,2:T(2,128)S(1)}, f32[2,8,64,128]{3,2,1,0:T(8,128)S(1)}, s32[]{:T(128)}) while((s32[]{:T(128)}, f32[2,8,64,128]{3,2,1,0:T(8,128)S(1)}, f32[2,8,1,1]{1,0,3,2:T(2,128)S(1)}, f32[2,8,64,128]{3,2,1,0:T(8,128)S(1)}, s32[]{:T(128)}) %tuple.45), condition=%wide.region_4.5_spmd, body=%wide.region_3.4_spmd.sunk | while | flops 262146 | bytes 3670181 | solution.py:77
  23.1 16.2 collective-permute-done.1
  40.7 12.8 collective-permute-done.1
  54.9 13.8 collective-permute-done.1
  70.2 12.1 collective-permute-done.1
  83.7 11.2 collective-permute-done.1
  131.5 11.9 collective-permute-done.1
  144.8 13.6 collective-permute-done.1
  159.9 15.1 collective-permute-done.1
  176.3 16.2 collective-permute-done.1
  194.0 17.3 collective-permute-done.1
  212.7 15.9 collective-permute-done.1
  230.0 15.1 collective-permute-done.1
  246.5 13.2 collective-permute-done.1
  261.2 12.4 collective-permute-done.1
  275.0 11.5 collective-permute-done.1
  322.9 11.5 collective-permute-done.1
  335.8 13.3 collective-permute-done.1
  350.5 14.8 collective-permute-done.1
  366.7 15.9 collective-permute-done.1
  384.1 17.2 collective-permute-done.1
  402.7 16.6 collective-permute-done.1
  420.7 14.8 collective-permute-done.1
  436.9 13.4 collective-permute-done.1
  451.7 12.5 collective-permute-done.1
  465.6 11.6 collective-permute-done.1
  513.8 11.2 collective-permute-done.1
  526.5 13.1 collective-permute-done.1
  541.0 22.3 collective-permute-done.1
  564.6 13.4 collective-permute-done.1
  591.4 11.3 collective-permute-done.1
  604.2 11.9 collective-permute-done.1
  617.5 13.9 collective-permute-done.1
  632.8 14.6 collective-permute-done.1
  648.9 15.8 collective-permute-done.1
  666.1 18.7 collective-permute-done.1
  686.2 17.1 collective-permute-done.1
  704.8 15.8 collective-permute-done.1
  722.0 15.7 collective-permute-done.1
  739.1 12.6 collective-permute-done.1
  753.2 14.5 collective-permute-done.1
  769.1 13.1 collective-permute-done.1
  783.6 14.4 collective-permute-done.1
  799.4 11.4 collective-permute-done.1
  823.8 12.0 collective-permute-done.1
  837.3 13.6 collective-permute-done.1
  852.3 14.6 collective-permute-done.1
  868.3 15.7 collective-permute-done.1
  885.4 18.2 collective-permute-done.1
  905.1 17.8 collective-permute-done.1
  924.3 15.9 collective-permute-done.1
  941.7 15.0 collective-permute-done.1
  957.6 972.8 %while.20 = (s32[]{:T(128)}, f32[2,8,64,128]{3,2,1,0:T(8,128)S(1)}, f32[2,8,1,1]{1,0,3,2:T(2,128)S(1)}, f32[2,8,64,128]{3,2,1,0:T(8,128)S(1)}, s32[]{:T(128)}) while((s32[]{:T(128)}, f32[2,8,64,128]{3,2,1,0:T(8,128)S(1)}, f32[2,8,1,1]{1,0,3,2:T(2,128)S(1)}, f32[2,8,64,128]{3,2,1,0:T(8,128)S(1)}, s32[]{:T(128)}) %tuple.46), condition=%wide.region_2.3_spmd, body=%wide.region_1.2_spmd.sunk | while | flops 262146 | bytes 3670181 | solution.py:76
  1076.1 11.3 collective-permute-done
  1269.4 11.2 collective-permute-done
  1380.9 19.7 collective-permute-start
  1535.1 11.7 collective-permute-done
  1606.4 14.2 collective-permute-start
  1750.4 11.2 collective-permute-done
  1765.9 11.3 collective-permute-done
  1783.3 11.1 collective-permute-done
  1835.5 11.3 collective-permute-done
  1854.4 11.2 collective-permute-done
  1936.3 320.8 %reduce-scatter.2.cloned.1.call-done = f32[2,2,8,128]{3,2,1,0:T(8,128)} async-done(((f32[2,2,64,128]{3,2,1,0:T(8,128)}), f32[2,2,8,128]{3,2,1,0:T(8,128)}) %reduce-scatter.2.cloned.1.call-update) | async-done | bytes 16400 | tf_op jit(solution)/shard_map/reduce_scatter | solution.py:91
  (355 shorter events, 1068.6 us)
Async XLA Ops:
  7.2 2249.9 %reduce-scatter.2.cloned.1.call-start = ((), (), s32[]{:S(2)}) async-start(), calls=%async_computation.1 | async-start | bytes 147456 | tf_op jit(solution)/shard_map/reduce_scatter | solution.py:91
  21.8 17.5 collective-permute-start.1
  53.6 15.1 collective-permute-start.1
  143.5 14.9 collective-permute-start.1
  158.6 16.4 collective-permute-start.1
  175.0 17.5 collective-permute-start.1
  192.6 18.6 collective-permute-start.1
  211.4 17.2 collective-permute-start.1
  228.7 16.4 collective-permute-start.1
  349.2 16.1 collective-permute-start.1
  365.4 17.2 collective-permute-start.1
  382.8 18.5 collective-permute-start.1
  401.4 17.9 collective-permute-start.1
  419.4 16.1 collective-permute-start.1
  539.6 23.6 %collective-permute-start.1 = (f32[2,8,64,128]{3,2,1,0:T(8,128)S(1)}, f32[2,8,64,128]{3,2,1,0:T(8,128)S(1)}, u32[]{:S(2)}, u32[]{:S(2)}) collective-permute-start(f32[2,8,64,128]{3,2,1,0:T(8,128)S(1)} %multiply_add_fusion.5), channel_id=1, source_target_pairs={{8,0},{16,8},{24,16},{32,24},{40,32},{48,40},{56,48},{64,56},{72,6... | collective-permute-start | bytes 1572872 | tf_op jit(solution)/shard_map/while/body/eval_jaxpr/ppermute | solution.py:10
  563.3 14.7 collective-permute-start.1
  616.2 15.2 collective-permute-start.1
  631.5 15.9 collective-permute-start.1
  647.6 17.1 collective-permute-start.1
  664.8 20.0 collective-permute-start.1
  684.9 18.5 collective-permute-start.1
  703.5 17.1 collective-permute-start.1
  720.7 17.0 collective-permute-start.1
  751.9 15.8 collective-permute-start.1
  782.3 15.7 collective-permute-start.1
  836.0 14.9 collective-permute-start.1
  851.0 15.9 collective-permute-start.1
  867.0 17.0 collective-permute-start.1
  884.1 19.5 collective-permute-start.1
  903.8 19.1 collective-permute-start.1
  923.0 17.2 collective-permute-start.1
  940.4 16.3 collective-permute-start.1
  981.0 14.8 collective-permute-start
  1037.0 17.8 collective-permute-start
  1055.0 16.8 collective-permute-start
  1071.9 15.5 collective-permute-start
  1087.5 20.9 collective-permute-start
  1108.5 15.4 collective-permute-start
  1229.5 15.9 collective-permute-start
  1245.5 17.0 collective-permute-start
  1262.6 18.1 collective-permute-start
  1280.8 18.0 collective-permute-start
  1298.9 15.6 collective-permute-start
  1380.9 27.5 %collective-permute-start = (f32[2,8,64,128]{3,2,1,0:T(8,128)S(1)}, f32[2,8,64,128]{3,2,1,0:T(8,128)S(1)}, u32[]{:S(2)}, u32[]{:S(2)}) collective-permute-start(f32[2,8,64,128]{3,2,1,0:T(8,128)S(1)} %multiply_add_fusion.4), channel_id=1, source_target_pairs={{0,8},{8,16},{16,24},{24,32},{32,40},{40,48},{48,56},{56,64},{64,7... | collective-permute-start | bytes 1572872 | tf_op jit(solution)/shard_map/while/body/eval_jaxpr/ppermute | solution.py:10
  1476.9 17.2 collective-permute-start
  1494.3 16.2 collective-permute-start
  1510.5 16.8 collective-permute-start
  1527.5 19.3 collective-permute-start
  1546.9 16.9 collective-permute-start
  1563.9 15.1 collective-permute-start
  1606.4 22.4 collective-permute-start
  1628.9 14.9 collective-permute-start
  1710.5 15.9 collective-permute-start
  1726.5 16.9 collective-permute-start
  1743.6 18.1 collective-permute-start
  1761.8 15.4 collective-permute-start
  1777.3 17.1 collective-permute-start
  1794.6 16.1 collective-permute-start
  1810.8 15.4 collective-permute-start
  1826.3 20.5 collective-permute-start
  1847.0 18.7 collective-permute-start
  1865.7 17.8 collective-permute-start
  1883.6 16.9 collective-permute-start
  1900.7 16.1 collective-permute-start
  (68 other events, 1769.6 us)
Sparse Core Ops, SparseCore 0:
  1932.1 324.9 reduce-scatter.1
where the time goes:
time: 2270 us; the launch traced here: 2260 us
  waiting for transfers between devices  1700 us (75%)
  starting transfers between devices  519 us (23%)
    ppermute x126, waiting for transfers between devices, shifted(): return lax.ppermute(block, axis, route)  1380 us
    ppermute x126, starting transfers between devices, shifted(): return lax.ppermute(block, axis, route)  519 us
    reduce_scatter x1, waiting for transfers between devices, shards(): lax.psum_scatter(jnp.stack([grad_key, grad_query]), 'head', scatter_dimen...  321 us
  transfers between devices with their start and end apart: 127, of which 127 were waited for; matrix products, arithmetic and copies ran while one was open for 0% of the time, Pallas kernels for 0%

commit v1 on v0

v1 whole, which is shorter than its diff:
```python
import functools

import jax
import jax.numpy as jnp
from jax import lax
from jax.experimental import pallas as pl
from jax.experimental.pallas import tpu as pltpu
from jax.sharding import PartitionSpec as P

MESH = pl.DeviceIdType.MESH
GROUP = 4
F32 = jnp.float32
BF16 = jnp.bfloat16


def dot(a, b):
    return lax.dot_general(a, b, (((1,), (0,)), ((), ())), preferred_element_type=F32)


def dot_nt(a, b):
    return lax.dot_general(a, b, (((1,), (1,)), ((), ())), preferred_element_type=F32)


def dot_tn(a, b):
    return lax.dot_general(a, b, (((0,), (0,)), ((), ())), preferred_element_type=F32)


def iota(shape, dim):
    return lax.broadcasted_iota(jnp.int32, shape, dim)


def kernel(
    sizes,
    values_ref, keys_ref, queries_ref, forget_ref, skip_ref, cot_ref,
    mixed_ref, gv_ref, gbc_ref,
    e_head, e_tail, s_val, s_cot, mix_acc, gv_acc, bc_acc,
    dx_send, dx_recv, dz_send, dz_recv,
    xin_send, xin_recv, zin_send, zin_recv, zout_send, zout_recv, xout_send, xout_recv,
    rs_send, rs_recv,
    send_sem, recv_sem,
):
    groups, peers = sizes
    seqs, rows, wide = values_ref.shape
    heads = forget_ref.shape[1]
    width = wide // heads
    state = keys_ref.shape[2]
    lanes = wide // GROUP
    piece = state // groups
    part = rows // peers
    streams = 2 * seqs

    me_seq = lax.axis_index("seq")
    me_head = lax.axis_index("head")
    me_x = lax.rem(me_seq, GROUP)
    me_g = me_seq // GROUP

    def x_peer(k):
        x = lax.rem(me_x + k, GROUP)
        return x, (me_g * GROUP + x, me_head)

    def z_peer(k):
        g = lax.rem(me_g + k, groups)
        return g, (g * GROUP + me_x, me_head)

    def h_peer(k):
        h = lax.rem(me_head + k, peers)
        return h, (me_seq, h)

    barrier = pltpu.get_barrier_semaphore()
    for peer, count in ((x_peer, GROUP), (z_peer, groups), (h_peer, peers)):
        for k in range(1, count):
            pl.semaphore_signal(barrier, 1, device_id=peer(k)[1], device_id_type=MESH)

    def copy(src, dst, slot, target):
        return pltpu.make_async_remote_copy(
            src_ref=src, dst_ref=dst, send_sem=send_sem.at[slot], recv_sem=recv_sem.at[slot],
            device_id=target, device_id_type=MESH,
        )

    def slot_of(phase, q):
        return 2 + phase * streams + q

    def spread(peer, count, src, dst, slot):
        for k in range(1, count):
            index, target = peer(k)
            copy(src(index), dst, slot, target).start()

    def arrived(buffer, count, slot):
        view = buffer.at[pl.ds(0, count - 1)]
        copy(view, view, slot, (me_seq, me_head)).wait_recv()

    def sent(buffer, count, slot):
        view = buffer.at[pl.ds(0, count - 1)]
        copy(view, view, slot, (me_seq, me_head)).wait_send()

    spread_heads = (iota((heads, wide), 1) // width == iota((heads, wide), 0)).astype(BF16)
    row2, col2 = iota((2 * rows, 2 * rows), 0), iota((2 * rows, 2 * rows), 1)
    upto = jnp.where(
        row2 < rows,
        (lax.rem(col2, rows) <= row2).astype(F32),
        (lax.rem(col2, rows) > row2 - rows).astype(F32),
    ).astype(BF16)
    row_w, lane_w = iota((rows, wide), 0), lax.rem(iota((rows, wide), 1), width)

    def decays(s):
        f = forget_ref[s]
        high = f.astype(BF16)
        low = (f - high.astype(F32)).astype(BF16)
        return dot_tn(high, spread_heads), dot_tn(low, spread_heads)

    fx = []
    for s in range(seqs):
        high, low = decays(s)
        fx.append((high, low))
        both = jnp.concatenate([high, low], axis=0).astype(BF16)
        sums = dot(upto, both)
        e_head[s] = jnp.exp(-sums[:rows])
        e_tail[s] = jnp.exp(-sums[rows:])
        total = jnp.exp(-sums[rows - 1 : rows])
        for j in range(GROUP):
            dx_send[j, s * 4 : s * 4 + 4] = jnp.broadcast_to(
                total[:, j * lanes : (j + 1) * lanes], (4, lanes)
            )
    dx_recv[me_x] = dx_send[me_x]
    pl.semaphore_wait(barrier, (GROUP - 1) + (groups - 1) + (peers - 1))
    spread(x_peer, GROUP, lambda i: dx_send.at[i], dx_recv.at[me_x], 0)
    for s in range(seqs):
        for back in range(2):
            q = 2 * s + back
            if back:
                scaled = (cot_ref[s].astype(F32) * e_head[s]).astype(BF16)
                s_cot[s] = scaled
                local = dot_tn(queries_ref[s], scaled)
            else:
                scaled = (values_ref[s].astype(F32) * e_tail[s]).astype(BF16)
                s_val[s] = scaled
                local = dot_tn(keys_ref[s], scaled)
            for j in range(GROUP):
                xin_send[q, j] = local[:, j * lanes : (j + 1) * lanes]
            spread(x_peer, GROUP, lambda i: xin_send.at[q, i], xin_recv.at[q, me_x], slot_of(0, q))
            xin_recv[q, me_x] = xin_send[q, me_x]

    def local_work(s):
        high, low = fx[s]
        zero = jnp.zeros((rows, wide), F32)

        def gap(keep, half):
            picked = jnp.concatenate(
                [jnp.where(keep, high, zero), jnp.where(keep, low, zero)], axis=0
            ).astype(BF16)
            return jnp.exp(-dot(half, picked))

        decay = jnp.where(lane_w <= row_w, gap(row_w > lane_w, upto[:rows]), 0.0)
        decay_t = jnp.where(lane_w >= row_w, gap(row_w <= lane_w, upto[rows:]), 0.0)
        keys, queries = keys_ref[s], queries_ref[s]
        keys2 = jnp.concatenate([keys, keys], axis=0)
        queries2 = jnp.concatenate([queries, queries], axis=0)
        copies = wide // (2 * rows)
        scores = jnp.concatenate([dot_nt(queries, keys2)] * copies, axis=1)
        scores_t = jnp.concatenate([dot_nt(keys, queries2)] * copies, axis=1)
        weights = (scores * decay).astype(BF16)
        weights_t = (scores_t * decay_t).astype(BF16)
        quad = 4 * width
        mask = (iota((quad, quad), 0) // rows == iota((quad, quad), 1) // width).astype(BF16)
        grad_sum = None
        for c in range(wide // quad):
            cols = slice(c * quad, (c + 1) * quad)
            val, cot = values_ref[s, :, cols], cot_ref[s, :, cols]
            val_diag = jnp.concatenate([val] * 4, axis=0) * mask
            cot_diag = jnp.concatenate([cot] * 4, axis=0) * mask
            skip_row = jnp.concatenate(
                [
                    jnp.where(
                        iota((1, 2 * width), 1) < width,
                        skip_ref[0, 4 * c + 2 * i],
                        skip_ref[0, 4 * c + 2 * i + 1],
                    )
                    for i in range(2)
                ],
                axis=1,
            )
            mix_acc[s, :, cols] = dot(weights[:, cols], val_diag) + skip_row * val.astype(F32)
            gv_acc[s, :, cols] = dot(weights_t[:, cols], cot_diag) + skip_row * cot.astype(F32)
            grad_w = dot_nt(cot, val_diag) * decay[:, cols]
            for i in range(2):
                term = grad_w[:, i * 2 * width : (i + 1) * 2 * width]
                grad_sum = term if grad_sum is None else grad_sum + term
        grad_sum = grad_sum.astype(BF16)
        bc_acc[2 * s] = dot(grad_sum, keys2)
        folded = dot_tn(grad_sum, queries)
        bc_acc[2 * s + 1] = folded[:rows] + folded[rows:]

    def decay_x(s, i):
        return dx_recv[i, 4 * s : 4 * s + 1]

    def decay_z(s, g):
        return dz_recv[g, 4 * s : 4 * s + 1]

    def group_total(q):
        s, back = q // 2, q % 2
        arrived(xin_recv.at[q], GROUP, slot_of(0, q))
        order = range(GROUP - 1, -1, -1) if back else range(GROUP)
        total = None
        for i in order:
            term = xin_recv[q, i]
            total = term if total is None else decay_x(s, i) * total + term
        zin_send[q] = total.reshape(groups, piece, lanes)
        spread(z_peer, groups, lambda g: zin_send.at[q, g], zin_recv.at[q, me_g], slot_of(1, q))
        zin_recv[q, me_g] = zin_send[q, me_g]

    def group_scan(q):
        s, back = q // 2, q % 2
        arrived(zin_recv.at[q], groups, slot_of(1, q))
        order = range(groups - 1, -1, -1) if back else range(groups)
        carry = jnp.zeros((piece, lanes), F32)
        for g in order:
            zout_send[q, g] = carry
            carry = decay_z(s, g) * carry + zin_recv[q, g]
        spread(z_peer, groups, lambda g: zout_send.at[q, g], zout_recv.at[q, me_g], slot_of(2, q))
        zout_recv[q, me_g] = zout_send[q, me_g]

    def member_scan(q):
        s, back = q // 2, q % 2
        arrived(zout_recv.at[q], groups, slot_of(2, q))
        order = range(GROUP - 1, -1, -1) if back else range(GROUP)
        carry = zout_recv[q].reshape(state, lanes)
        for n, i in enumerate(order):
            xout_send[q, i] = carry
            if n < GROUP - 1:
                carry = decay_x(s, i) * carry + xin_recv[q, i]
        spread(x_peer, GROUP, lambda i: xout_send.at[q, i], xout_recv.at[q, me_x], slot_of(3, q))
        xout_recv[q, me_x] = xout_send[q, me_x]

    def finish(q):
        s, back = q // 2, q % 2
        arrived(xout_recv.at[q], GROUP, slot_of(3, q))
        carried = jnp.concatenate([xout_recv[q, j] for j in range(GROUP)], axis=1).astype(BF16)
        if back:
            grad = bc_acc[2 * s + 1] + dot_nt(s_val[s], carried)
        else:
            grad = bc_acc[2 * s] + dot_nt(s_cot[s], carried)
        rs_send[q] = grad.reshape(peers, part, state)
        spread(h_peer, peers, lambda h: rs_send.at[q, h], rs_recv.at[q, me_head], slot_of(4, q))
        rs_recv[q, me_head] = rs_send[q, me_head]
        if back:
            gv_ref[s] = (gv_acc[s] + e_tail[s] * dot(keys_ref[s], carried)).astype(BF16)
        else:
            mixed_ref[s] = (mix_acc[s] + e_head[s] * dot(queries_ref[s], carried)).astype(BF16)

    def reduce_heads(q):
        s, back = q // 2, q % 2
        arrived(rs_recv.at[q], peers, slot_of(4, q))
        total = rs_recv[q, 0]
        for h in range(1, peers):
            total = total + rs_recv[q, h]
        gbc_ref[1 - back, s] = total

    arrived(dx_recv, GROUP, 0)
    product = dx_recv[0]
    for i in range(1, GROUP):
        product = product * dx_recv[i]
    dz_send[...] = product
    spread(z_peer, groups, lambda g: dz_send, dz_recv.at[me_g], 1)
    dz_recv[me_g] = product
    local_work(0)
    group_total(0)
    group_total(1)
    local_work(1)
    arrived(dz_recv, groups, 1)
    group_scan(0)
    group_total(2)
    group_scan(1)
    group_total(3)
    member_scan(0)
    group_scan(2)
    member_scan(1)
    group_scan(3)
    finish(0)
    member_scan(2)
    finish(1)
    member_scan(3)
    finish(2)
    reduce_heads(0)
    reduce_heads(1)
    finish(3)
    reduce_heads(2)
    reduce_heads(3)

    sent(dx_send, GROUP, 0)
    sent(dz_recv, groups, 1)
    for q in range(streams):
        sent(xin_send.at[q], GROUP, slot_of(0, q))
        sent(zin_send.at[q], groups, slot_of(1, q))
        sent(zout_send.at[q], groups, slot_of(2, q))
        sent(xout_send.at[q], GROUP, slot_of(3, q))
        sent(rs_send.at[q], peers, slot_of(4, q))


def solution(mesh):
    blocks, peers = mesh.shape["seq"], mesh.shape["head"]
    groups = blocks // GROUP

    def shards(values, keys_b, queries_c, forget, skip, cotangent):
        seqs, rows, wide = values.shape
        state = keys_b.shape[-1]
        streams = 2 * seqs
        lanes, piece, part = wide // GROUP, state // groups, rows // peers
        slots = 2 + 5 * streams
        vmem = pl.BlockSpec(memory_space=pltpu.VMEM)
        smem = pl.BlockSpec(memory_space=pltpu.SMEM)
        return pl.pallas_call(
            functools.partial(kernel, (groups, peers)),
            out_shape=(
                jax.ShapeDtypeStruct(values.shape, BF16),
                jax.ShapeDtypeStruct(values.shape, BF16),
                jax.ShapeDtypeStruct((2, seqs, part, state), F32),
            ),
            in_specs=[vmem, vmem, vmem, vmem, smem, vmem],
            out_specs=(vmem, vmem, vmem),
            scratch_shapes=[
                pltpu.VMEM((seqs, rows, wide), F32),
                pltpu.VMEM((seqs, rows, wide), F32),
                pltpu.VMEM((seqs, rows, wide), BF16),
                pltpu.VMEM((seqs, rows, wide), BF16),
                pltpu.VMEM((seqs, rows, wide), F32),
                pltpu.VMEM((seqs, rows, wide), F32),
                pltpu.VMEM((2 * seqs, rows, state), F32),
                pltpu.VMEM((GROUP, 4 * seqs, lanes), F32),
                pltpu.VMEM((GROUP, 4 * seqs, lanes), F32),
                pltpu.VMEM((4 * seqs, lanes), F32),
                pltpu.VMEM((groups, 4 * seqs, lanes), F32),
                pltpu.VMEM((streams, GROUP, state, lanes), F32),
                pltpu.VMEM((streams, GROUP, state, lanes), F32),
                pltpu.VMEM((streams, groups, piece, lanes), F32),
                pltpu.VMEM((streams, groups, piece, lanes), F32),
                pltpu.VMEM((streams, groups, piece, lanes), F32),
                pltpu.VMEM((streams, groups, piece, lanes), F32),
                pltpu.VMEM((streams, GROUP, state, lanes), F32),
                pltpu.VMEM((streams, GROUP, state, lanes), F32),
                pltpu.VMEM((streams, peers, part, state), F32),
                pltpu.VMEM((streams, peers, part, state), F32),
                pltpu.SemaphoreType.DMA((slots,)),
                pltpu.SemaphoreType.DMA((slots,)),
            ],
            compiler_params=pltpu.CompilerParams(collective_id=0, has_side_effects=True),
        )(values, keys_b, queries_c, forget, skip.reshape(1, -1), cotangent)

    in_specs = (
        P(None, "seq", "head"),
        P(None, "seq", None),
        P(None, "seq", None),
        P(None, "head", "seq"),
        P("head"),
        P(None, "seq", "head"),
    )
    out_specs = (
        P(None, "seq", "head"),
        P(None, "seq", "head"),
        P(None, None, ("seq", "head"), None),
    )
    return jax.shard_map(shards, mesh=mesh, in_specs=in_specs, out_specs=out_specs, check_vma=False)
```

time: 2270 us -> 57.4 us (0.03)
  waiting for transfers between devices: 1700 us -> 0 us
  starting transfers between devices: 519 us -> 0 us
  Pallas kernels: 0 us -> 53.6 us
    ppermute x126 -> x0, waiting for transfers between devices: 1380 us -> none  [shifted(): return lax.ppermute(block, axis, route)]
    ppermute x126 -> x0, starting transfers between devices: 519 us -> none  [shifted(): return lax.ppermute(block, axis, route)]
    reduce_scatter x1 -> x0, waiting for transfers between devices: 321 us -> none  [shards(): lax.psum_scatter(jnp.stack([grad_key, grad_query]), 'head', scatter_dimen...]
    pallas_call x0 -> x1, Pallas kernels: none -> 53.6 us  [shards(): pl.pallas_call(functools.partial(kernel, (groups, peers)), out_shape=(jax...]
  transfers between devices with their start and end apart: 127 -> 0, of which waited for: 127 -> 0; matrix products, arithmetic and copies ran while one was open for 0% -> 0% of each run, Pallas kernels for 0% -> 0%
where the time goes in v1:
time: 57.4 us; the launch traced here: 57.2 us
  Pallas kernels  53.6 us (93%)
  local copies, waits for them, and re-layouts  2.93 us (5%)
  between operations  0.65 us (1%)
    pallas_call x1, Pallas kernels, shards(): pl.pallas_call(functools.partial(kernel, (groups, peers)), out_shape=(jax...  53.6 us
    unnamed x7, local copies, waits for them, and re-layouts  2.93 us

profile of v1, /device:TPU:1, one launch (start us, length us, event | category | flops | bytes accessed | tf_op | source)
XLA Modules:
  0.0 57.2 jit_solution(6685638731737154550)
XLA Ops:
  0.6 53.6 %shard_map.85 = (bf16[2,64,512]{2,1,0:T(8,128)(2,1)}, bf16[2,64,512]{2,1,0:T(8,128)(2,1)}, f32[2,2,8,128]{3,2,1,0:T(8,128)}) custom-call(bf16[2,64,512]{2,1,0:T(8,128)(2,1)} %values_ref.1, bf16[2,64,128]{2,1,0:T(8,128)(2,1)} %keys_ref.1, bf16[2,64,128]{2,1,0:T(8,128)(2,1)} %queries_ref.1, f32[2,8,64]{2,1,0:T(8,128)} %forget_ref.1, f32[1,8]{1,0:T(1,128)} %bitcast.1, ...), custom_call_target="tpu_custom_call" | custom-call | tf_op jit(solution)/shard_map/pallas_call | solution.py:311
  54.2 0.0 copy-start
  54.3 1.6 %copy.12 = bf16[2,64,512]{2,1,0:T(8,128)(2,1)} copy(bf16[2,64,512]{2,1,0:T(8,128)(2,1)} %get-tuple-element.6) | data formatting | bytes 262144
  55.9 0.0 copy-done
  55.9 0.0 copy-start.1
  55.9 0.7 %copy.13 = bf16[2,64,512]{2,1,0:T(8,128)(2,1)} copy(bf16[2,64,512]{2,1,0:T(8,128)(2,1)S(1)} %copy-done) | data formatting | bytes 262144
  56.5 0.1 copy-done.1
  56.6 0.6 %copy.14 = f32[2,2,8,128]{3,2,1,0:T(8,128)} copy(f32[2,2,8,128]{3,2,1,0:T(8,128)S(1)} %copy-done.1) | data formatting | bytes 32768
Async XLA Ops:
  54.2 1.6 %copy-start = (bf16[2,64,512]{2,1,0:T(8,128)(2,1)S(1)}, bf16[2,64,512]{2,1,0:T(8,128)(2,1)}, u32[]{:S(2)}) copy-start(bf16[2,64,512]{2,1,0:T(8,128)(2,1)} %get-tuple-element.7) | copy-start | bytes 393220
  55.9 0.7 %copy-start.1 = (f32[2,2,8,128]{3,2,1,0:T(8,128)S(1)}, f32[2,2,8,128]{3,2,1,0:T(8,128)}, u32[]{:S(2)}) copy-start(f32[2,2,8,128]{3,2,1,0:T(8,128)} %get-tuple-element.8) | copy-start | bytes 49156

commit v2 on v1

v2 whole, which is shorter than its diff:
```python
import functools

import jax
import jax.numpy as jnp
from jax import lax
from jax.experimental import pallas as pl
from jax.experimental.pallas import tpu as pltpu
from jax.sharding import PartitionSpec as P

MESH = pl.DeviceIdType.MESH
GROUP = 4
F32 = jnp.float32
BF16 = jnp.bfloat16


def dot(a, b):
    return lax.dot_general(a, b, (((1,), (0,)), ((), ())), preferred_element_type=F32)


def dot_nt(a, b):
    return lax.dot_general(a, b, (((1,), (1,)), ((), ())), preferred_element_type=F32)


def dot_tn(a, b):
    return lax.dot_general(a, b, (((0,), (0,)), ((), ())), preferred_element_type=F32)


def iota(shape, dim):
    return lax.broadcasted_iota(jnp.int32, shape, dim)


ORDER = (
    ("T", 0), ("T", 1), ("L", 1), ("T", 2), ("T", 3), ("D", 0), ("S", 0), ("T", 4), ("S", 1), ("T", 5),
    ("S", 2), ("T", 6), ("S", 3), ("T", 7), ("M", 0), ("S", 4), ("M", 1), ("S", 5), ("M", 2), ("S", 6),
    ("M", 3), ("S", 7), ("M", 4), ("F", 0), ("M", 5), ("M", 6), ("F", 1), ("M", 7), ("F", 2), ("R", 0),
    ("R", 1), ("F", 3), ("R", 2), ("R", 3),
)


def kernel(
    sizes,
    values_in, keys_in, queries_in, forget_in, skip_in, cot_in,
    mixed_out, gv_out, gbc_out,
    values_ref, keys_ref, queries_ref, forget_ref, skip_ref, cot_ref,
    mixed_ref, gv_ref, gbc_ref,
    e_head, e_tail, s_val, s_cot, mix_acc, gv_acc, bc_acc,
    dx_send, dx_recv, dz_send, dz_recv,
    xin_send, xin_recv, zin_send, zin_recv, zout_send, zout_recv, xout_send, xout_recv,
    rs_send, rs_recv,
    send_sem, recv_sem, load_sem, round_sem, write_sem,
):
    groups, peers = sizes
    seqs, rows, wide = values_ref.shape
    heads = forget_ref.shape[1]
    width = wide // heads
    state = keys_ref.shape[2]
    lanes = wide // GROUP
    half = state // 2
    piece = state // groups
    depth = groups // 2
    part = rows // peers

    me_seq = lax.axis_index("seq")
    me_head = lax.axis_index("head")
    me_x = lax.rem(me_seq, GROUP)
    me_g = me_seq // GROUP
    me_y, me_z = me_g // depth, lax.rem(me_g, depth)
    parity, me_piece = lax.rem(me_g, 2), me_g // 2

    loads = [
        pltpu.make_async_copy(src, dst, load_sem.at[n])
        for n, (src, dst) in enumerate(
            (
                (forget_in, forget_ref), (keys_in, keys_ref), (values_in, values_ref),
                (queries_in, queries_ref), (cot_in, cot_ref), (skip_in, skip_ref),
            )
        )
    ]
    for load in loads:
        load.start()

    def at_x(x):
        return (me_g * GROUP + x, me_head)

    def at_group(g):
        return (g * GROUP + me_x, me_head)

    x_peers = [lax.rem(me_x + k, GROUP) for k in (2, 1, 3)]
    away = sorted(
        ((dy, dz) for dy in range(2) for dz in range(depth) if dy or dz),
        key=lambda d: -(d[0] + min(d[1], depth - d[1])),
    )
    z_peers = [
        lax.rem(me_y + dy, 2) * depth + lax.rem(me_z + dz, depth) for dy, dz in away
    ]
    cores = 2 if peers % 2 == 0 else 1
    ring = peers // cores
    me_r, me_c = me_head // cores, lax.rem(me_head, cores)
    h_away = sorted(
        ((dr, dc) for dr in range(ring) for dc in range(cores) if dr or dc),
        key=lambda d: -min(d[0], ring - d[0]),
    )
    h_peers = [
        lax.rem(me_r + dr, ring) * cores + lax.rem(me_c + dc, cores) for dr, dc in h_away
    ]

    def steps(size, *distances):
        return sorted({d % size for d in distances} - {0})

    def z_near(*distances):
        return [
            at_group(me_y * depth + lax.rem(me_z + d, depth)) for d in steps(depth, *distances)
        ]

    y_other = [at_group((1 - me_y) * depth + me_z)]
    core_other = [(me_seq, me_r * cores + 1 - me_c)] if cores == 2 else []
    h_near = core_other + [
        (me_seq, lax.rem(me_r + d, ring) * cores + me_c) for d in steps(ring, 1, -1)
    ]
    barrier = pltpu.get_barrier_semaphore()
    near = [at_x(x) for x in x_peers] + h_near + y_other + z_near(1, -1)
    for target in near:
        pl.semaphore_signal(barrier, 1, device_id=target, device_id_type=MESH)
    rounds = (z_near(1, -1) + y_other, z_near(2, -2), y_other, h_near, core_other)

    def tell(n):
        for target in rounds[n]:
            pl.semaphore_signal(round_sem.at[n], 1, device_id=target, device_id_type=MESH)

    def told(n):
        if rounds[n]:
            pl.semaphore_wait(round_sem.at[n], len(rounds[n]))

    def copy(src, dst, send, recv, target):
        return pltpu.make_async_remote_copy(
            src_ref=src, dst_ref=dst, send_sem=send_sem.at[send], recv_sem=recv_sem.at[recv],
            device_id=target, device_id_type=MESH,
        )

    streams = 2 * seqs
    X_IN, Z_IN, Z_OUT, X_OUT, HEADS = range(2, 7)
    x_in, z_in, z_out, x_out, heads_in = (
        2, 2 + 2 * streams, 2 + 3 * streams, 2 + 5 * streams, 2 + 6 * streams
    )

    def arrived(view, slot):
        copy(view, view, slot, slot, (me_seq, me_head)).wait_recv()

    def sent(view, slot):
        copy(view, view, slot, slot, (me_seq, me_head)).wait_send()

    every = seqs * wide
    lane_head = iota((seqs * heads, every), 1) // width
    spread_heads = (lane_head == iota((seqs * heads, every), 0)).astype(BF16)
    row2, col2 = iota((2 * rows, 2 * rows), 0), iota((2 * rows, 2 * rows), 1)
    upto = jnp.where(
        row2 < rows,
        (lax.rem(col2, rows) <= row2).astype(F32),
        (lax.rem(col2, rows) > row2 - rows).astype(F32),
    ).astype(BF16)
    row_w, lane_w = iota((rows, wide), 0), lax.rem(iota((rows, wide), 1), width)

    loads[0].wait()
    flat = forget_ref[...].reshape(seqs * heads, rows)
    high = flat.astype(BF16)
    low = (flat - high.astype(F32)).astype(BF16)
    high, low = dot_tn(high, spread_heads), dot_tn(low, spread_heads)
    sums = dot(upto, jnp.concatenate([high, low], axis=0).astype(BF16))
    for s in range(seqs):
        cols = slice(s * wide, (s + 1) * wide)
        e_head[s] = jnp.exp(-sums[:rows, cols])
        e_tail[s] = jnp.exp(-sums[rows:, cols])
        total = jnp.exp(-sums[rows - 1 : rows, cols])
        for j in range(GROUP):
            dx_send[j, s : s + 1] = total[:, j * lanes : (j + 1) * lanes]
    dx_recv[me_x] = dx_send[me_x]

    def local_state(q):
        s, back = q // 2, q % 2
        if back:
            scaled = (cot_ref[s].astype(F32) * e_head[s]).astype(BF16)
            s_cot[s] = scaled
            local = dot_tn(queries_ref[s], scaled)
        else:
            scaled = (values_ref[s].astype(F32) * e_tail[s]).astype(BF16)
            s_val[s] = scaled
            local = dot_tn(keys_ref[s], scaled)
        for j in range(GROUP):
            xin_send[q, j] = local[:, j * lanes : (j + 1) * lanes]

    def half_rows(h):
        return pl.ds(h * half, half)

    def send_state(q):
        for h in range(2):
            for x in x_peers:
                copy(
                    xin_send.at[q, x, half_rows(h)], xin_recv.at[q, me_x, half_rows(h)],
                    X_IN, x_in + 2 * q + h, at_x(x),
                ).start()
        xin_recv[q, me_x] = xin_send[q, me_x]

    loads[1].wait()
    loads[2].wait()
    local_state(0)
    pl.semaphore_wait(barrier, len(near))
    tell(0)
    tell(3)
    for x in x_peers:
        copy(dx_send.at[x], dx_recv.at[me_x], 0, 0, at_x(x)).start()
    send_state(0)
    for load in loads[3:]:
        load.wait()
    for q in range(1, 2 * seqs):
        local_state(q)
        send_state(q)

    def local_work(s):
        mine = slice(s * wide, (s + 1) * wide)
        zero = jnp.zeros((rows, wide), F32)

        def gap(keep, span):
            picked = jnp.concatenate(
                [jnp.where(keep, high[:, mine], zero), jnp.where(keep, low[:, mine], zero)], axis=0
            ).astype(BF16)
            return jnp.exp(-dot(span, picked))

        decay = jnp.where(lane_w <= row_w, gap(row_w > lane_w, upto[:rows]), 0.0)
        decay_t = jnp.where(lane_w >= row_w, gap(row_w <= lane_w, upto[rows:]), 0.0)
        keys, queries = keys_ref[s], queries_ref[s]
        keys2 = jnp.concatenate([keys, keys], axis=0)
        queries2 = jnp.concatenate([queries, queries], axis=0)
        copies = wide // (2 * rows)
        scores = jnp.concatenate([dot_nt(queries, keys2)] * copies, axis=1)
        scores_t = jnp.concatenate([dot_nt(keys, queries2)] * copies, axis=1)
        weights = (scores * decay).astype(BF16)
        weights_t = (scores_t * decay_t).astype(BF16)
        quad = 4 * width
        mask = (iota((quad, quad), 0) // rows == iota((quad, quad), 1) // width).astype(BF16)
        grad_sum = None
        for c in range(wide // quad):
            cols = slice(c * quad, (c + 1) * quad)
            val, cot = values_ref[s, :, cols], cot_ref[s, :, cols]
            val_diag = jnp.concatenate([val] * 4, axis=0) * mask
            cot_diag = jnp.concatenate([cot] * 4, axis=0) * mask
            skip_row = jnp.concatenate(
                [
                    jnp.broadcast_to(skip_ref[0:1, 4 * c + i : 4 * c + i + 1], (1, width))
                    for i in range(4)
                ],
                axis=1,
            )
            mix_acc[s, :, cols] = dot(weights[:, cols], val_diag) + skip_row * val.astype(F32)
            gv_acc[s, :, cols] = dot(weights_t[:, cols], cot_diag) + skip_row * cot.astype(F32)
            grad_w = dot_nt(cot, val_diag) * decay[:, cols]
            for i in range(2):
                term = grad_w[:, i * 2 * width : (i + 1) * 2 * width]
                grad_sum = term if grad_sum is None else grad_sum + term
        grad_sum = grad_sum.astype(BF16)
        bc_acc[2 * s] = dot(grad_sum, keys2)
        folded = dot_tn(grad_sum, queries)
        bc_acc[2 * s + 1] = folded[:rows] + folded[rows:]

    def decay_x(s, i):
        return dx_recv[i, s : s + 1]

    def decay_z(s, g):
        return dz_recv[g, s : s + 1]

    def group_total(q, h):
        s, back = q // 2, q % 2
        arrived(xin_recv.at[q, pl.ds(0, GROUP - 1), half_rows(h)], x_in + 2 * q + h)
        order = range(GROUP - 1, -1, -1) if back else range(GROUP)
        total = None
        for i in order:
            term = xin_recv[q, i, half_rows(h)]
            total = term if total is None else decay_x(s, i) * total + term
        zin_send[q, h] = total.reshape(depth, piece, lanes)
        first = lax.rem(me_z + h, 2)

        def send(dy, k):
            g = lax.rem(me_y + dy, 2) * depth + lax.rem(me_z + first + 2 * k, depth)
            copy(
                zin_send.at[q, h, g // 2], zin_recv.at[q, me_g],
                Z_IN, z_in + q, at_group(g),
            ).start()

        hops = sorted(range(depth // 2), key=lambda k: -min(2 * k + 1, depth - 2 * k))
        for dy, k in [(1, k) for k in hops] + [(0, k) for k in hops if k]:
            send(dy, k)

        @pl.when(parity != h)
        def _():
            send(0, 0)

        @pl.when(parity == h)
        def _():
            zin_recv[q, me_g] = zin_send[q, h, me_piece]

    def group_scan(q, h):
        s, back = q // 2, q % 2

        @pl.when(parity == h)
        def _():
            arrived(zin_recv.at[q, pl.ds(0, groups - 1)], z_in + q)
            order = range(groups - 1, -1, -1) if back else range(groups)
            carry = jnp.zeros((piece, lanes), F32)
            for n, g in enumerate(order):
                zout_send[q, g] = carry
                if n < groups - 1:
                    carry = decay_z(s, g) * carry + zin_recv[q, g]
            for g in z_peers:
                copy(
                    zout_send.at[q, g], zout_recv.at[q, h, me_piece],
                    Z_OUT, z_out + 2 * q + h, at_group(g),
                ).start()
            zout_recv[q, h, me_piece] = zout_send[q, me_g]

    def member_scan(q, h):
        s, back = q // 2, q % 2

        @pl.when(parity != h)
        def _():
            arrived(zout_recv.at[q, h], z_out + 2 * q + h)

        @pl.when(parity == h)
        def _():
            arrived(zout_recv.at[q, h, pl.ds(0, depth - 1)], z_out + 2 * q + h)

        order = range(GROUP - 1, -1, -1) if back else range(GROUP)
        carry = zout_recv[q, h].reshape(half, lanes)
        for n, i in enumerate(order):
            xout_send[q, i, half_rows(h)] = carry
            if n < GROUP - 1:
                carry = decay_x(s, i) * carry + xin_recv[q, i, half_rows(h)]
        for x in x_peers:
            copy(
                xout_send.at[q, x, half_rows(h)], xout_recv.at[q, me_x, half_rows(h)],
                X_OUT, x_out + q, at_x(x),
            ).start()
        xout_recv[q, me_x, half_rows(h)] = xout_send[q, me_x, half_rows(h)]

    written = []

    def finish(q):
        s, back = q // 2, q % 2
        arrived(xout_recv.at[q, pl.ds(0, GROUP - 1)], x_out + q)
        carried = jnp.concatenate([xout_recv[q, j] for j in range(GROUP)], axis=1).astype(BF16)
        if back:
            grad = bc_acc[2 * s + 1] + dot_nt(s_val[s], carried)
        else:
            grad = bc_acc[2 * s] + dot_nt(s_cot[s], carried)
        rs_send[q] = grad.reshape(peers, part, state)
        for p in h_peers:
            copy(
                rs_send.at[q, p], rs_recv.at[q, me_head], HEADS, heads_in + q, (me_seq, p)
            ).start()
        rs_recv[q, me_head] = rs_send[q, me_head]
        if back:
            gv_ref[s] = (gv_acc[s] + e_tail[s] * dot(keys_ref[s], carried)).astype(BF16)
        else:
            mixed_ref[s] = (mix_acc[s] + e_head[s] * dot(queries_ref[s], carried)).astype(BF16)
        source, result = (gv_ref, gv_out) if back else (mixed_ref, mixed_out)
        written.append(pltpu.make_async_copy(source.at[s], result.at[s], write_sem.at[q]))
        written[-1].start()

    def reduce_heads(q):
        s, back = q // 2, q % 2
        arrived(rs_recv.at[q, pl.ds(0, peers - 1)], heads_in + q)
        total = rs_recv[q, 0]
        for h in range(1, peers):
            total = total + rs_recv[q, h]
        gbc_ref[1 - back, s] = total

    local_work(0)
    for n in range(3):
        told(n)
        if n < 2:
            tell(n + 1)
    told(3)
    tell(4)
    arrived(dx_recv.at[pl.ds(0, GROUP - 1)], 0)
    product = dx_recv[0]
    for i in range(1, GROUP):
        product = product * dx_recv[i]
    dz_send[...] = product
    for g in z_peers:
        copy(dz_send, dz_recv.at[me_g], 1, 1, at_group(g)).start()
    dz_recv[me_g] = product
    told(4)
    chunks = [(q, h) for q in range(2 * seqs) for h in range(2)]

    def run(order):
        for kind, at in order:
            if kind == "T":
                group_total(*chunks[at])
            elif kind == "L":
                local_work(at)
            elif kind == "D":
                arrived(dz_recv.at[pl.ds(0, groups - 1)], 1)
            elif kind == "S":
                group_scan(*chunks[at])
            elif kind == "M":
                member_scan(*chunks[at])
            elif kind == "F":
                finish(at)
            else:
                reduce_heads(at)

    run(ORDER)
    last = pltpu.make_async_copy(gbc_ref, gbc_out, write_sem.at[2 * seqs])
    last.start()
    sent(dx_send.at[pl.ds(0, GROUP - 1)], 0)
    sent(dz_recv.at[pl.ds(0, groups - 1)], 1)
    sent(xin_send.at[:, pl.ds(0, GROUP - 1)], X_IN)
    sent(zin_recv.at[:, pl.ds(0, groups - 1)], Z_IN)
    sent(zout_send.at[:, pl.ds(0, groups - 1)], Z_OUT)
    sent(xout_send.at[:, pl.ds(0, GROUP - 1)], X_OUT)
    sent(rs_send.at[:, pl.ds(0, peers - 1)], HEADS)
    for result in written:
        result.wait()
    last.wait()


def write_out(*refs):
    count = len(refs) // 2
    sources, results, sem = refs[:count], refs[count : 2 * count], refs[-1]
    copies = [
        pltpu.make_async_copy(a, b, sem.at[n]) for n, (a, b) in enumerate(zip(sources, results))
    ]
    for each in copies:
        each.start()
    for each in copies:
        each.wait()


def solution(mesh):
    blocks, peers = mesh.shape["seq"], mesh.shape["head"]
    groups = blocks // GROUP

    def shards(values, keys_b, queries_c, forget, skip, cotangent):
        seqs, rows, wide = values.shape
        state = keys_b.shape[-1]
        streams = 2 * seqs
        lanes, piece, part = wide // GROUP, state // groups, rows // peers
        anywhere = pl.BlockSpec(memory_space=pl.ANY)
        args = (values, keys_b, queries_c, forget, skip.reshape(1, -1), cotangent)
        results = (
            (values.shape, BF16),
            (values.shape, BF16),
            ((2, seqs, part, state), F32),
        )
        inner = pl.pallas_call(
            functools.partial(kernel, (groups, peers)),
            out_shape=tuple(pltpu.VMEM(*r) for r in results),
            in_specs=[anywhere] * len(args),
            out_specs=(anywhere,) * len(results),
            scratch_shapes=[pltpu.VMEM(a.shape, a.dtype) for a in args]
            + [pltpu.VMEM(*r) for r in results]
            + [
                pltpu.VMEM((seqs, rows, wide), F32),
                pltpu.VMEM((seqs, rows, wide), F32),
                pltpu.VMEM((seqs, rows, wide), BF16),
                pltpu.VMEM((seqs, rows, wide), BF16),
                pltpu.VMEM((seqs, rows, wide), F32),
                pltpu.VMEM((seqs, rows, wide), F32),
                pltpu.VMEM((2 * seqs, rows, state), F32),
                pltpu.VMEM((GROUP, seqs, lanes), F32),
                pltpu.VMEM((GROUP, seqs, lanes), F32),
                pltpu.VMEM((seqs, lanes), F32),
                pltpu.VMEM((groups, seqs, lanes), F32),
                pltpu.VMEM((streams, GROUP, state, lanes), F32),
                pltpu.VMEM((streams, GROUP, state, lanes), F32),
                pltpu.VMEM((streams, 2, groups // 2, piece, lanes), F32),
                pltpu.VMEM((streams, groups, piece, lanes), F32),
                pltpu.VMEM((streams, groups, piece, lanes), F32),
                pltpu.VMEM((streams, 2, groups // 2, piece, lanes), F32),
                pltpu.VMEM((streams, GROUP, state, lanes), F32),
                pltpu.VMEM((streams, GROUP, state, lanes), F32),
                pltpu.VMEM((streams, peers, part, state), F32),
                pltpu.VMEM((streams, peers, part, state), F32),
                pltpu.SemaphoreType.DMA((7,)),
                pltpu.SemaphoreType.DMA((2 + 7 * streams,)),
                pltpu.SemaphoreType.DMA((len(args),)),
                pltpu.SemaphoreType.REGULAR((5,)),
                pltpu.SemaphoreType.DMA((streams + 1,)),
            ],
            compiler_params=pltpu.CompilerParams(collective_id=0, has_side_effects=True),
        )(*args)
        return pl.pallas_call(
            write_out,
            out_shape=tuple(jax.ShapeDtypeStruct(*r) for r in results),
            in_specs=[anywhere] * len(results),
            out_specs=(anywhere,) * len(results),
            scratch_shapes=[pltpu.SemaphoreType.DMA((len(results),))],
        )(*[pltpu.with_memory_space_constraint(x, pltpu.VMEM) for x in inner])

    in_specs = (
        P(None, "seq", "head"),
        P(None, "seq", None),
        P(None, "seq", None),
        P(None, "head", "seq"),
        P("head"),
        P(None, "seq", "head"),
    )
    out_specs = (
        P(None, "seq", "head"),
        P(None, "seq", "head"),
        P(None, None, ("seq", "head"), None),
    )
    return jax.shard_map(shards, mesh=mesh, in_specs=in_specs, out_specs=out_specs, check_vma=False)
```

time: 57.4 us -> 50.3 us (0.88)
  Pallas kernels: 53.6 us -> 49.5 us
  local copies, waits for them, and re-layouts: 2.93 us -> 0 us
    pallas_call x1 -> x2, Pallas kernels: 53.6 us -> 49.5 us  [the longest x1 48.8 us: shards(): pl.pallas_call(functools.partial(kernel, (groups, peers)), out_shape=tupl...]
    unnamed x7 -> x0, local copies, waits for them, and re-layouts: 2.93 us -> none
where the time goes in v2:
time: 50.3 us; the launch traced here: 50.2 us
  Pallas kernels  49.5 us (98%)
  between operations  0.64 us (1%)
    pallas_call x1, Pallas kernels, shards(): pl.pallas_call(functools.partial(kernel, (groups, peers)), out_shape=tupl...  48.8 us

profile of v2, /device:TPU:1, one launch (start us, length us, event | category | flops | bytes accessed | tf_op | source)
XLA Modules:
  0.0 50.2 jit_solution(13711838615588903658)
XLA Ops:
  0.6 48.8 %shard_map.85 = (bf16[2,64,512]{2,1,0:T(8,128)(2,1)S(1)}, bf16[2,64,512]{2,1,0:T(8,128)(2,1)S(1)}, f32[2,2,8,128]{3,2,1,0:T(8,128)S(1)}) custom-call(bf16[2,64,512]{2,1,0:T(8,128)(2,1)} %values_in.1, bf16[2,64,128]{2,1,0:T(8,128)(2,1)} %keys_in.1, bf16[2,64,128]{2,1,0:T(8,128)(2,1)} %queries_in.1, f32[2,8,64]{2,1,0:T(8,128)} %forget_in.1, f32[1,8]{1,0:T(1,128)} %bitcast.1, ...), custom_call_target="tpu_custom_call" | custom-call | tf_op jit(solution)/shard_map/pallas_call | solution.py:453
  49.5 0.7 %shard_map.86 = (bf16[2,64,512]{2,1,0:T(8,128)(2,1)}, bf16[2,64,512]{2,1,0:T(8,128)(2,1)}, f32[2,2,8,128]{3,2,1,0:T(8,128)}) custom-call(bf16[2,64,512]{2,1,0:T(8,128)(2,1)S(1)} %get-tuple-element.6.refs_0_, bf16[2,64,512]{2,1,0:T(8,128)(2,1)S(1)} %get-tuple-element.7.refs_1_, f32[2,2,8,128]{3,2,1,0:T(8,128)S(1)} %get-tuple-element.8.refs_2_), custom_call_target="tpu_custom_call" | custom-call | tf_op jit(solution)/shard_map/pallas_call | solution.py:490

commit v3 on v2

--- a/solution.py
+++ b/solution.py
@@ -30,10 +30,10 @@
 
 
 ORDER = (
-    ("T", 0), ("T", 1), ("L", 1), ("T", 2), ("T", 3), ("D", 0), ("S", 0), ("T", 4), ("S", 1), ("T", 5),
+    ("T", 0), ("L", 0), ("T", 1), ("L", 1), ("T", 2), ("T", 3), ("D", 0), ("S", 0), ("T", 4), ("S", 1), ("T", 5),
     ("S", 2), ("T", 6), ("S", 3), ("T", 7), ("M", 0), ("S", 4), ("M", 1), ("S", 5), ("M", 2), ("S", 6),
-    ("M", 3), ("S", 7), ("M", 4), ("F", 0), ("M", 5), ("M", 6), ("F", 1), ("M", 7), ("F", 2), ("R", 0),
-    ("R", 1), ("F", 3), ("R", 2), ("R", 3),
+    ("M", 3), ("S", 7), ("M", 4), ("F", 0), ("M", 5), ("M", 6), ("M", 7), ("F", 1), ("F", 2), ("F", 3),
+    ("R", 0), ("R", 1), ("R", 2), ("R", 3),
 )
 
 
@@ -372,18 +372,18 @@
             total = total + rs_recv[q, h]
         gbc_ref[1 - back, s] = total
 
-    local_work(0)
-    for n in range(3):
-        told(n)
-        if n < 2:
-            tell(n + 1)
-    told(3)
-    tell(4)
+    told(0)
+    tell(1)
     arrived(dx_recv.at[pl.ds(0, GROUP - 1)], 0)
     product = dx_recv[0]
     for i in range(1, GROUP):
         product = product * dx_recv[i]
     dz_send[...] = product
+    told(1)
+    tell(2)
+    told(3)
+    tell(4)
+    told(2)
     for g in z_peers:
         copy(dz_send, dz_recv.at[me_g], 1, 1, at_group(g)).start()
     dz_recv[me_g] = product

time: 50.3 us -> 49.5 us (0.984)
  Pallas kernels: 49.5 us -> 48.7 us
    pallas_call x1, Pallas kernels: 48.8 us -> 48 us  [shards(): pl.pallas_call(functools.partial(kernel, (groups, peers)), out_shape=tupl...]
where the time goes in v3:
time: 49.5 us; the launch traced here: 49.4 us
  Pallas kernels  48.7 us (98%)
  between operations  0.64 us (1%)
    pallas_call x1, Pallas kernels, shards(): pl.pallas_call(functools.partial(kernel, (groups, peers)), out_shape=tupl...  48 us

profile of v3, /device:TPU:1, one launch (start us, length us, event | category | flops | bytes accessed | tf_op | source)
XLA Modules:
  0.0 49.4 jit_solution(9520980465803768243)
XLA Ops:
  0.6 48.0 %shard_map.85 = (bf16[2,64,512]{2,1,0:T(8,128)(2,1)S(1)}, bf16[2,64,512]{2,1,0:T(8,128)(2,1)S(1)}, f32[2,2,8,128]{3,2,1,0:T(8,128)S(1)}) custom-call(bf16[2,64,512]{2,1,0:T(8,128)(2,1)} %values_in.1, bf16[2,64,128]{2,1,0:T(8,128)(2,1)} %keys_in.1, bf16[2,64,128]{2,1,0:T(8,128)(2,1)} %queries_in.1, f32[2,8,64]{2,1,0:T(8,128)} %forget_in.1, f32[1,8]{1,0:T(1,128)} %bitcast.1, ...), custom_call_target="tpu_custom_call" | custom-call | tf_op jit(solution)/shard_map/pallas_call | solution.py:453
  48.6 0.7 %shard_map.86 = (bf16[2,64,512]{2,1,0:T(8,128)(2,1)}, bf16[2,64,512]{2,1,0:T(8,128)(2,1)}, f32[2,2,8,128]{3,2,1,0:T(8,128)}) custom-call(bf16[2,64,512]{2,1,0:T(8,128)(2,1)S(1)} %get-tuple-element.6.refs_0_, bf16[2,64,512]{2,1,0:T(8,128)(2,1)S(1)} %get-tuple-element.7.refs_1_, f32[2,2,8,128]{3,2,1,0:T(8,128)S(1)} %get-tuple-element.8.refs_2_), custom_call_target="tpu_custom_call" | custom-call | tf_op jit(solution)/shard_map/pallas_call | solution.py:490

commit v4 on v3

v4 whole, which is shorter than its diff:
```python
import functools

import jax
import jax.numpy as jnp
from jax import lax
from jax.experimental import pallas as pl
from jax.experimental.pallas import tpu as pltpu
from jax.sharding import PartitionSpec as P

MESH = pl.DeviceIdType.MESH
GROUP = 4
F32 = jnp.float32
BF16 = jnp.bfloat16


def dot(a, b):
    return lax.dot_general(a, b, (((1,), (0,)), ((), ())), preferred_element_type=F32)


def dot_nt(a, b):
    return lax.dot_general(a, b, (((1,), (1,)), ((), ())), preferred_element_type=F32)


def dot_tn(a, b):
    return lax.dot_general(a, b, (((0,), (0,)), ((), ())), preferred_element_type=F32)


def iota(shape, dim):
    return lax.broadcasted_iota(jnp.int32, shape, dim)


ORDER = (
    ("K", 0), ("I", 1), ("B", 0), ("I", 2), ("K", 1), ("T", 0), ("B", 1), ("I", 3), ("L", 0), ("T", 1),
    ("B", 2), ("L", 1), ("T", 2), ("B", 3), ("D", 0), ("S", 0), ("T", 3), ("S", 1), ("S", 2), ("S", 3),
    ("K", 2), ("M", 0), ("M", 1), ("C", 0), ("M", 2), ("C", 1), ("M", 3), ("C", 2), ("C", 3), ("F", 0),
    ("Z", 0), ("F", 1), ("Z", 1), ("Z", 2), ("F", 2), ("F", 3), ("Z", 3),
)


def kernel(
    sizes,
    values_in, keys_in, queries_in, forget_in, skip_in, cot_in,
    mixed_out, gv_out, gbc_out,
    values_ref, keys_ref, queries_ref, forget_ref, skip_ref, cot_ref,
    mixed_ref, gv_ref, gbc_ref,
    e_head, e_tail, mix_acc, gv_acc, bc_acc,
    dx_send, dx_recv, dz_send, dz_recv,
    map_send, maps, slice_send, slices, states,
    zin_send, zin_recv, zout_send, zout_recv, cross_send, cross,
    grads, pair_recv, sums_send, sums_recv,
    send_sem, recv_sem, load_sem, round_sem, write_sem,
):
    groups, peers = sizes
    seqs, rows, wide = values_ref.shape
    heads = forget_ref.shape[1]
    width = wide // heads
    state = keys_ref.shape[2]
    lanes = wide // GROUP
    piece = state // groups
    depth = groups // 2
    part = rows // peers

    me_seq = lax.axis_index("seq")
    me_head = lax.axis_index("head")
    me_x = lax.rem(me_seq, GROUP)
    me_g = me_seq // GROUP
    me_y, me_z = me_g // depth, lax.rem(me_g, depth)

    loads = [
        pltpu.make_async_copy(src, dst, load_sem.at[n])
        for n, (src, dst) in enumerate(
            (
                (forget_in, forget_ref), (keys_in, keys_ref), (values_in, values_ref),
                (queries_in, queries_ref), (cot_in, cot_ref), (skip_in, skip_ref),
            )
        )
    ]
    for load in loads:
        load.start()

    def at_x(x):
        return (me_g * GROUP + x, me_head)

    def at_group(g):
        return (g * GROUP + me_x, me_head)

    x_peers = [lax.rem(me_x + k, GROUP) for k in (2, 1, 3)]
    away = sorted(
        ((dy, dz) for dy in range(2) for dz in range(depth) if dy or dz),
        key=lambda d: -(d[0] + min(d[1], depth - d[1])),
    )
    z_peers = [
        lax.rem(me_y + dy, 2) * depth + lax.rem(me_z + dz, depth) for dy, dz in away
    ]
    cores = 2
    ring = peers // cores
    share = rows // cores
    me_r, me_c = me_head // cores, lax.rem(me_head, cores)
    far = sorted(
        ((dr, dx) for dr in range(ring) for dx in range(GROUP) if dr or dx),
        key=lambda d: -(2 * min(d[0], ring - d[0]) + min(d[1], GROUP - d[1])),
    )
    members = [(lax.rem(me_r + dr, ring), lax.rem(me_x + dx, GROUP)) for dr, dx in far]

    def at_member(r, x):
        return (me_g * GROUP + x, r * cores + me_c)

    def at_ring(r):
        return (me_seq, r * cores + me_c)

    def steps(size, *distances):
        return sorted({d % size for d in distances} - {0})

    def z_near(*distances):
        return [
            at_group(me_y * depth + lax.rem(me_z + d, depth)) for d in steps(depth, *distances)
        ]

    y_other = [at_group((1 - me_y) * depth + me_z)]
    core_other = (me_seq, me_r * cores + 1 - me_c)
    r_near = [at_ring(lax.rem(me_r + d, ring)) for d in steps(ring, 1, -1)]
    barrier = pltpu.get_barrier_semaphore()
    near = [at_x(x) for x in x_peers] + [core_other] + r_near + y_other + z_near(1, -1, 2, -2)
    for target in near:
        pl.semaphore_signal(barrier, 1, device_id=target, device_id_type=MESH)
    r_far = [at_ring(lax.rem(me_r + 2, ring))] if ring > 3 else []
    rounds = (z_near(2, -2) + y_other, y_other, r_near, r_far)

    def tell(n):
        for target in rounds[n]:
            pl.semaphore_signal(round_sem.at[n], 1, device_id=target, device_id_type=MESH)

    def told(n):
        if rounds[n]:
            pl.semaphore_wait(round_sem.at[n], len(rounds[n]))

    def copy(src, dst, send, recv, target):
        return pltpu.make_async_remote_copy(
            src_ref=src, dst_ref=dst, send_sem=send_sem.at[send], recv_sem=recv_sem.at[recv],
            device_id=target, device_id_type=MESH,
        )

    streams = 2 * seqs
    MAPS, PASSED, SLICES, Z_IN, Z_OUT, CROSS, PAIR, SUMS = range(2, 10)

    def slot(phase, q):
        return 2 + (phase - 2) * streams + q

    def arrived(view, at):
        copy(view, view, at, at, (me_seq, me_head)).wait_recv()

    def sent(view, at):
        copy(view, view, at, at, (me_seq, me_head)).wait_send()

    every = seqs * wide
    lane_head = iota((seqs * heads, every), 1) // width
    spread_heads = (lane_head == iota((seqs * heads, every), 0)).astype(BF16)
    row2, col2 = iota((2 * rows, 2 * rows), 0), iota((2 * rows, 2 * rows), 1)
    upto = jnp.where(
        row2 < rows,
        (lax.rem(col2, rows) <= row2).astype(F32),
        (lax.rem(col2, rows) > row2 - rows).astype(F32),
    ).astype(BF16)
    row_w, lane_w = iota((rows, wide), 0), lax.rem(iota((rows, wide), 1), width)

    loads[0].wait()
    flat = forget_ref[...].reshape(seqs * heads, rows)
    high = flat.astype(BF16)
    low = (flat - high.astype(F32)).astype(BF16)
    high, low = dot_tn(high, spread_heads), dot_tn(low, spread_heads)
    sums = dot(upto, jnp.concatenate([high, low], axis=0).astype(BF16))
    for s in range(seqs):
        cols = slice(s * wide, (s + 1) * wide)
        e_head[s] = jnp.exp(-sums[:rows, cols])
        e_tail[s] = jnp.exp(-sums[rows:, cols])
        total = jnp.exp(-sums[rows - 1 : rows, cols])
        for j in range(GROUP):
            dx_send[j, s : s + 1] = total[:, j * lanes : (j + 1) * lanes]
    dx_recv[me_x] = dx_send[me_x]

    mine = pl.ds(pl.multiple_of(me_c * share, share), share)

    def send_inputs(q):
        s, back = q // 2, q % 2
        map_ref, input_ref, scale = (
            (queries_ref, cot_ref, e_head) if back else (keys_ref, values_ref, e_tail)
        )
        map_send[q] = map_ref[s].astype(F32)
        scaled = input_ref[s].astype(F32) * scale[s]
        for j in range(GROUP):
            slice_send[q, j] = scaled[:, j * lanes : (j + 1) * lanes]
        if q == 0:
            pl.semaphore_wait(barrier, len(near))
            tell(0)
            tell(2)
            for x in x_peers:
                copy(dx_send.at[x], dx_recv.at[me_x], 0, 0, at_x(x)).start()
        for x in x_peers:
            copy(
                map_send.at[q, mine], maps.at[q, me_x, mine], MAPS, slot(MAPS, q), at_x(x)
            ).start()
        for x in x_peers:
            copy(
                slice_send.at[q, x], slices.at[q, me_x], SLICES, slot(SLICES, q), at_x(x)
            ).start()
        maps[q, me_x, mine] = map_send[q, mine]
        slices[q, me_x] = slice_send[q, me_x]

    loads[1].wait()
    loads[2].wait()
    send_inputs(0)
    for load in loads[3:]:
        load.wait()

    def local_work(s):
        own = slice(s * wide, (s + 1) * wide)
        zero = jnp.zeros((rows, wide), F32)

        def gap(keep, span):
            picked = jnp.concatenate(
                [jnp.where(keep, high[:, own], zero), jnp.where(keep, low[:, own], zero)], axis=0
            ).astype(BF16)
            return jnp.exp(-dot(span, picked))

        decay = jnp.where(lane_w <= row_w, gap(row_w > lane_w, upto[:rows]), 0.0)
        decay_t = jnp.where(lane_w >= row_w, gap(row_w <= lane_w, upto[rows:]), 0.0)
        keys, queries = keys_ref[s], queries_ref[s]
        keys2 = jnp.concatenate([keys, keys], axis=0)
        queries2 = jnp.concatenate([queries, queries], axis=0)
        copies = wide // (2 * rows)
        scores = jnp.concatenate([dot_nt(queries, keys2)] * copies, axis=1)
        scores_t = jnp.concatenate([dot_nt(keys, queries2)] * copies, axis=1)
        weights = (scores * decay).astype(BF16)
        weights_t = (scores_t * decay_t).astype(BF16)
        quad = 4 * width
        mask = (iota((quad, quad), 0) // rows == iota((quad, quad), 1) // width).astype(BF16)
        grad_sum = None
        for c in range(wide // quad):
            cols = slice(c * quad, (c + 1) * quad)
            val, cot = values_ref[s, :, cols], cot_ref[s, :, cols]
            val_diag = jnp.concatenate([val] * 4, axis=0) * mask
            cot_diag = jnp.concatenate([cot] * 4, axis=0) * mask
            skip_row = jnp.concatenate(
                [
                    jnp.broadcast_to(skip_ref[0:1, 4 * c + i : 4 * c + i + 1], (1, width))
                    for i in range(4)
                ],
                axis=1,
            )
            mix_acc[s, :, cols] = dot(weights[:, cols], val_diag) + skip_row * val.astype(F32)
            gv_acc[s, :, cols] = dot(weights_t[:, cols], cot_diag) + skip_row * cot.astype(F32)
            grad_w = dot_nt(cot, val_diag) * decay[:, cols]
            for i in range(2):
                term = grad_w[:, i * 2 * width : (i + 1) * 2 * width]
                grad_sum = term if grad_sum is None else grad_sum + term
        grad_sum = grad_sum.astype(BF16)
        bc_acc[2 * s] = dot(grad_sum, keys2)
        folded = dot_tn(grad_sum, queries)
        bc_acc[2 * s + 1] = folded[:rows] + folded[rows:]

    def decay_x(s, i):
        return dx_recv[i, s : s + 1]

    def decay_z(s, g):
        return dz_recv[g, s : s + 1]

    def pass_maps(q):
        arrived(maps.at[q, pl.ds(0, GROUP - 1), pl.ds(0, share)], slot(MAPS, q))
        view = maps.at[q, pl.ds(0, GROUP), mine]
        copy(view, view, PASSED, slot(PASSED, q), core_other).start()

    def group_total(q):
        s, back = q // 2, q % 2
        arrived(slices.at[q, pl.ds(0, GROUP - 1)], slot(SLICES, q))
        arrived(maps.at[q, pl.ds(0, GROUP), pl.ds(0, share)], slot(PASSED, q))
        weighted, weight = [None] * GROUP, None
        for i in range(GROUP) if back else range(GROUP - 1, -1, -1):
            weighted[i] = slices[q, i] if weight is None else weight * slices[q, i]
            weight = decay_x(s, i) if weight is None else weight * decay_x(s, i)
        all_maps = maps[q].reshape(GROUP * rows, state).astype(BF16)
        total = dot_tn(all_maps, jnp.concatenate(weighted, axis=0).astype(BF16))
        zin_send[q] = total.reshape(groups, piece, lanes)
        for g in z_peers:
            copy(
                zin_send.at[q, g], zin_recv.at[q, me_g], Z_IN, slot(Z_IN, q), at_group(g)
            ).start()
        zin_recv[q, me_g] = zin_send[q, me_g]
        for i in range(1, GROUP) if back else range(GROUP - 1):
            states[q, i] = dot_tn(maps[q, i].astype(BF16), slices[q, i].astype(BF16))

    def group_scan(q):
        s, back = q // 2, q % 2
        arrived(zin_recv.at[q, pl.ds(0, groups - 1)], slot(Z_IN, q))
        order = range(groups - 1, -1, -1) if back else range(groups)
        carry = jnp.zeros((piece, lanes), F32)
        for n, g in enumerate(order):
            zout_send[q, g] = carry
            if n < groups - 1:
                carry = decay_z(s, g) * carry + zin_recv[q, g]
        for g in z_peers:
            copy(
                zout_send.at[q, g], zout_recv.at[q, me_g], Z_OUT, slot(Z_OUT, q), at_group(g)
            ).start()
        zout_recv[q, me_g] = zout_send[q, me_g]

    def member_scan(q):
        s, back = q // 2, q % 2
        other = q - 1 if back else q + 1
        arrived(zout_recv.at[q, pl.ds(0, groups - 1)], slot(Z_OUT, q))
        order = range(GROUP - 1, -1, -1) if back else range(GROUP)
        carry = zout_recv[q].reshape(state, lanes)
        carried = [None] * GROUP
        for n, i in enumerate(order):
            carried[i] = carry.astype(BF16)
            grad = dot_nt(slices[other, i].astype(BF16), carried[i])
            grad = grad.reshape(ring, cores, part, state)
            for c in range(cores):
                grads[q, c, :, i] = grad[:, c]
            if n < GROUP - 1:
                carry = decay_x(s, i) * carry + states[q, i]
        own = bc_acc[2 * s + back].reshape(ring, cores, part, state)
        for c in range(cores):
            grads[q, c, :, me_x] = grads[q, c, :, me_x] + own[:, c]
        copy(grads.at[q, 1 - me_c], pair_recv.at[q], PAIR, slot(PAIR, q), core_other).start()
        for i in order:
            cross_send[q, i] = dot(maps[other, i].astype(BF16), carried[i])
        for x in x_peers:
            copy(
                cross_send.at[q, x], cross.at[q, me_x], CROSS, slot(CROSS, q), at_x(x)
            ).start()
        cross[q, me_x] = cross_send[q, me_x]

    def sum_pair(q):
        arrived(pair_recv.at[q], slot(PAIR, q))
        sums_send[q] = grads[q, me_c] + pair_recv[q]
        me = me_r * GROUP + me_x
        for r, x in members:
            copy(
                sums_send.at[q, r, x], sums_recv.at[q, me], SUMS, slot(SUMS, q), at_member(r, x)
            ).start()
        sums_recv[q, me] = sums_send[q, me_r, me_x]

    def sum_all(q):
        s, back = q // 2, q % 2
        arrived(sums_recv.at[q, pl.ds(0, len(members))], slot(SUMS, q))
        total = sums_recv[q, 0]
        for n in range(1, ring * GROUP):
            total = total + sums_recv[q, n]
        gbc_ref[1 - back, s] = total

    written = []

    def finish(q):
        s, back = q // 2, q % 2
        arrived(cross.at[q, pl.ds(0, GROUP - 1)], slot(CROSS, q))
        terms = jnp.concatenate([cross[q, j] for j in range(GROUP)], axis=1)
        if back:
            gv_ref[s] = (gv_acc[s] + e_tail[s] * terms).astype(BF16)
        else:
            mixed_ref[s] = (mix_acc[s] + e_head[s] * terms).astype(BF16)
        source, result = (gv_ref, gv_out) if back else (mixed_ref, mixed_out)
        written.append(pltpu.make_async_copy(source.at[s], result.at[s], write_sem.at[q]))
        written[-1].start()

    def hear_near():
        told(0)
        tell(1)
        told(2)
        tell(3)

    def group_decays():
        arrived(dx_recv.at[pl.ds(0, GROUP - 1)], 0)
        product = dx_recv[0]
        for i in range(1, GROUP):
            product = product * dx_recv[i]
        dz_send[...] = product
        dz_recv[me_g] = product
        told(1)
        for g in z_peers:
            copy(dz_send, dz_recv.at[me_g], 1, 1, at_group(g)).start()

    def all_decays():
        arrived(dz_recv.at[pl.ds(0, groups - 1)], 1)

    work = {
        "I": send_inputs, "B": pass_maps, "T": group_total, "S": group_scan, "M": member_scan, "C": sum_pair,
        "Z": sum_all, "F": finish, "L": local_work,
        "K": lambda n: (hear_near, group_decays, lambda: told(3))[n](), "D": lambda _: all_decays(),
    }

    def run(order):
        for kind, at in order:
            work[kind](at)

    run(ORDER)
    last = pltpu.make_async_copy(gbc_ref, gbc_out, write_sem.at[2 * seqs])
    last.start()
    sent(dx_send.at[pl.ds(0, GROUP - 1)], 0)
    sent(dz_recv.at[pl.ds(0, groups - 1)], 1)
    sent(maps.at[:, pl.ds(0, GROUP - 1), pl.ds(0, share)], MAPS)
    sent(maps.at[:, :, pl.ds(0, share)], PASSED)
    sent(slices.at[:, pl.ds(0, GROUP - 1)], SLICES)
    sent(zin_recv.at[:, pl.ds(0, groups - 1)], Z_IN)
    sent(zout_recv.at[:, pl.ds(0, groups - 1)], Z_OUT)
    sent(cross.at[:, pl.ds(0, GROUP - 1)], CROSS)
    sent(pair_recv, PAIR)
    sent(sums_recv.at[:, pl.ds(0, len(members))], SUMS)
    for result in written:
        result.wait()
    last.wait()


def write_out(*refs):
    count = len(refs) // 2
    sources, results, sem = refs[:count], refs[count : 2 * count], refs[-1]
    copies = [
        pltpu.make_async_copy(a, b, sem.at[n]) for n, (a, b) in enumerate(zip(sources, results))
    ]
    for each in copies:
        each.start()
    for each in copies:
        each.wait()


def solution(mesh):
    blocks, peers = mesh.shape["seq"], mesh.shape["head"]
    groups = blocks // GROUP

    def shards(values, keys_b, queries_c, forget, skip, cotangent):
        seqs, rows, wide = values.shape
        state = keys_b.shape[-1]
        streams = 2 * seqs
        lanes, piece, part = wide // GROUP, state // groups, rows // peers
        anywhere = pl.BlockSpec(memory_space=pl.ANY)
        args = (values, keys_b, queries_c, forget, skip.reshape(1, -1), cotangent)
        results = (
            (values.shape, BF16),
            (values.shape, BF16),
            ((2, seqs, part, state), F32),
        )
        inner = pl.pallas_call(
            functools.partial(kernel, (groups, peers)),
            out_shape=tuple(pltpu.VMEM(*r) for r in results),
            in_specs=[anywhere] * len(args),
            out_specs=(anywhere,) * len(results),
            scratch_shapes=[pltpu.VMEM(a.shape, a.dtype) for a in args]
            + [pltpu.VMEM(*r) for r in results]
            + [
                *[pltpu.VMEM((seqs, rows, wide), F32)] * 4,
                pltpu.VMEM((2 * seqs, rows, state), F32),
                *[pltpu.VMEM((GROUP, seqs, lanes), F32)] * 2,
                pltpu.VMEM((seqs, lanes), F32),
                pltpu.VMEM((groups, seqs, lanes), F32),
                pltpu.VMEM((streams, rows, state), F32),
                pltpu.VMEM((streams, GROUP, rows, state), F32),
                *[pltpu.VMEM((streams, GROUP, rows, lanes), F32)] * 2,
                pltpu.VMEM((streams, GROUP, state, lanes), F32),
                *[pltpu.VMEM((streams, groups, piece, lanes), F32)] * 4,
                *[pltpu.VMEM((streams, GROUP, rows, lanes), F32)] * 2,
                pltpu.VMEM((streams, 2, peers // 2, GROUP, part, state), F32),
                *[pltpu.VMEM((streams, peers // 2, GROUP, part, state), F32)] * 2,
                pltpu.VMEM((streams, peers // 2 * GROUP, part, state), F32),
                pltpu.SemaphoreType.DMA((10,)),
                pltpu.SemaphoreType.DMA((2 + 8 * streams,)),
                pltpu.SemaphoreType.DMA((len(args),)),
                pltpu.SemaphoreType.REGULAR((4,)),
                pltpu.SemaphoreType.DMA((streams + 1,)),
            ],
            compiler_params=pltpu.CompilerParams(collective_id=0, has_side_effects=True),
        )(*args)
        return pl.pallas_call(
            write_out,
            out_shape=tuple(jax.ShapeDtypeStruct(*r) for r in results),
            in_specs=[anywhere] * len(results),
            out_specs=(anywhere,) * len(results),
            scratch_shapes=[pltpu.SemaphoreType.DMA((len(results),))],
        )(*[pltpu.with_memory_space_constraint(x, pltpu.VMEM) for x in inner])

    in_specs = (
        P(None, "seq", "head"),
        P(None, "seq", None),
        P(None, "seq", None),
        P(None, "head", "seq"),
        P("head"),
        P(None, "seq", "head"),
    )
    out_specs = (
        P(None, "seq", "head"),
        P(None, "seq", "head"),
        P(None, None, ("seq", "head"), None),
    )
    return jax.shard_map(shards, mesh=mesh, in_specs=in_specs, out_specs=out_specs, check_vma=False)
```

time: 49.5 us -> 47 us (0.949)
  Pallas kernels: 48.7 us -> 46.2 us
    pallas_call x1, Pallas kernels: 48 us -> 45.5 us  [shards(): pl.pallas_call(functools.partial(kernel, (groups, peers)), out_shape=tupl...]
where the time goes in v4:
time: 47 us; the launch traced here: 46.8 us
  Pallas kernels  46.2 us (98%)
  between operations  0.64 us (1%)
    pallas_call x1, Pallas kernels, shards(): pl.pallas_call(functools.partial(kernel, (groups, peers)), out_shape=tupl...  45.5 us

profile of v4, /device:TPU:1, one launch (start us, length us, event | category | flops | bytes accessed | tf_op | source)
XLA Modules:
  0.0 46.8 jit_solution(14126940752873555487)
XLA Ops:
  0.6 45.5 %shard_map.85 = (bf16[2,64,512]{2,1,0:T(8,128)(2,1)S(1)}, bf16[2,64,512]{2,1,0:T(8,128)(2,1)S(1)}, f32[2,2,8,128]{3,2,1,0:T(8,128)S(1)}) custom-call(bf16[2,64,512]{2,1,0:T(8,128)(2,1)} %values_in.1, bf16[2,64,128]{2,1,0:T(8,128)(2,1)} %keys_in.1, bf16[2,64,128]{2,1,0:T(8,128)(2,1)} %queries_in.1, f32[2,8,64]{2,1,0:T(8,128)} %forget_in.1, f32[1,8]{1,0:T(1,128)} %bitcast.1, ...), custom_call_target="tpu_custom_call" | custom-call | tf_op jit(solution)/shard_map/pallas_call | solution.py:441
  46.1 0.7 %shard_map.86 = (bf16[2,64,512]{2,1,0:T(8,128)(2,1)}, bf16[2,64,512]{2,1,0:T(8,128)(2,1)}, f32[2,2,8,128]{3,2,1,0:T(8,128)}) custom-call(bf16[2,64,512]{2,1,0:T(8,128)(2,1)S(1)} %get-tuple-element.6.refs_0_, bf16[2,64,512]{2,1,0:T(8,128)(2,1)S(1)} %get-tuple-element.7.refs_1_, f32[2,2,8,128]{3,2,1,0:T(8,128)S(1)} %get-tuple-element.8.refs_2_), custom_call_target="tpu_custom_call" | custom-call | tf_op jit(solution)/shard_map/pallas_call | solution.py:471

commit v5 on v4

--- a/solution.py
+++ b/solution.py
@@ -32,8 +32,9 @@
 ORDER = (
     ("K", 0), ("I", 1), ("B", 0), ("I", 2), ("K", 1), ("T", 0), ("B", 1), ("I", 3), ("L", 0), ("T", 1),
     ("B", 2), ("L", 1), ("T", 2), ("B", 3), ("D", 0), ("S", 0), ("T", 3), ("S", 1), ("S", 2), ("S", 3),
-    ("K", 2), ("M", 0), ("M", 1), ("C", 0), ("M", 2), ("C", 1), ("M", 3), ("C", 2), ("C", 3), ("F", 0),
-    ("Z", 0), ("F", 1), ("Z", 1), ("Z", 2), ("F", 2), ("F", 3), ("Z", 3),
+    ("K", 2), ("M", 0), ("Y", 0), ("M", 1), ("C", 0), ("Y", 1), ("M", 2), ("C", 1), ("Y", 2), ("C", 2),
+    ("M", 3), ("C", 3), ("Y", 3), ("F", 0), ("Z", 0), ("F", 1), ("Z", 1), ("Z", 2), ("F", 2), ("F", 3),
+    ("Z", 3),
 )
 
 
@@ -45,7 +46,7 @@
     mixed_ref, gv_ref, gbc_ref,
     e_head, e_tail, mix_acc, gv_acc, bc_acc,
     dx_send, dx_recv, dz_send, dz_recv,
-    map_send, maps, slice_send, slices, states,
+    map_send, maps, slice_send, slices, states, states_out,
     zin_send, zin_recv, zout_send, zout_recv, cross_send, cross,
     grads, pair_recv, sums_send, sums_recv,
     send_sem, recv_sem, load_sem, round_sem, write_sem,
@@ -70,8 +71,8 @@
         pltpu.make_async_copy(src, dst, load_sem.at[n])
         for n, (src, dst) in enumerate(
             (
-                (forget_in, forget_ref), (keys_in, keys_ref), (values_in, values_ref),
-                (queries_in, queries_ref), (cot_in, cot_ref), (skip_in, skip_ref),
+                (forget_in, forget_ref), (queries_in, queries_ref), (cot_in, cot_ref),
+                (keys_in, keys_ref), (values_in, values_ref), (skip_in, skip_ref),
             )
         )
     ]
@@ -146,6 +147,9 @@
     def slot(phase, q):
         return 2 + (phase - 2) * streams + q
 
+    def each_total(q, g):
+        return 2 + 8 * streams + (q // 2) * groups + g
+
     def arrived(view, at):
         copy(view, view, at, at, (me_seq, me_head)).wait_recv()
 
@@ -181,14 +185,11 @@
     mine = pl.ds(pl.multiple_of(me_c * share, share), share)
 
     def send_inputs(q):
-        s, back = q // 2, q % 2
+        s, back = q // 2, 1 - q % 2
         map_ref, input_ref, scale = (
             (queries_ref, cot_ref, e_head) if back else (keys_ref, values_ref, e_tail)
         )
         map_send[q] = map_ref[s].astype(F32)
-        scaled = input_ref[s].astype(F32) * scale[s]
-        for j in range(GROUP):
-            slice_send[q, j] = scaled[:, j * lanes : (j + 1) * lanes]
         if q == 0:
             pl.semaphore_wait(barrier, len(near))
             tell(0)
@@ -199,6 +200,9 @@
             copy(
                 map_send.at[q, mine], maps.at[q, me_x, mine], MAPS, slot(MAPS, q), at_x(x)
             ).start()
+        scaled = input_ref[s].astype(F32) * scale[s]
+        for j in range(GROUP):
+            slice_send[q, j] = scaled[:, j * lanes : (j + 1) * lanes]
         for x in x_peers:
             copy(
                 slice_send.at[q, x], slices.at[q, me_x], SLICES, slot(SLICES, q), at_x(x)
@@ -270,7 +274,7 @@
         copy(view, view, PASSED, slot(PASSED, q), core_other).start()
 
     def group_total(q):
-        s, back = q // 2, q % 2
+        s, back = q // 2, 1 - q % 2
         arrived(slices.at[q, pl.ds(0, GROUP - 1)], slot(SLICES, q))
         arrived(maps.at[q, pl.ds(0, GROUP), pl.ds(0, share)], slot(PASSED, q))
         weighted, weight = [None] * GROUP, None
@@ -280,38 +284,59 @@
         all_maps = maps[q].reshape(GROUP * rows, state).astype(BF16)
         total = dot_tn(all_maps, jnp.concatenate(weighted, axis=0).astype(BF16))
         zin_send[q] = total.reshape(groups, piece, lanes)
+        at = slot(Z_IN, q) if back else each_total(q, me_g)
         for g in z_peers:
-            copy(
-                zin_send.at[q, g], zin_recv.at[q, me_g], Z_IN, slot(Z_IN, q), at_group(g)
-            ).start()
+            copy(zin_send.at[q, g], zin_recv.at[q, me_g], Z_IN, at, at_group(g)).start()
         zin_recv[q, me_g] = zin_send[q, me_g]
         for i in range(1, GROUP) if back else range(GROUP - 1):
             states[q, i] = dot_tn(maps[q, i].astype(BF16), slices[q, i].astype(BF16))
 
-    def group_scan(q):
-        s, back = q // 2, q % 2
-        arrived(zin_recv.at[q, pl.ds(0, groups - 1)], slot(Z_IN, q))
-        order = range(groups - 1, -1, -1) if back else range(groups)
-        carry = jnp.zeros((piece, lanes), F32)
-        for n, g in enumerate(order):
-            zout_send[q, g] = carry
-            if n < groups - 1:
-                carry = decay_z(s, g) * carry + zin_recv[q, g]
-        for g in z_peers:
+    def carry_out(q, g):
+        @pl.when(me_g != g)
+        def _():
             copy(
                 zout_send.at[q, g], zout_recv.at[q, me_g], Z_OUT, slot(Z_OUT, q), at_group(g)
             ).start()
-        zout_recv[q, me_g] = zout_send[q, me_g]
+
+        @pl.when(me_g == g)
+        def _():
+            zout_recv[q, g] = zout_send[q, g]
+
+    def one_total(q, g):
+        @pl.when(me_g != g)
+        def _():
+            arrived(zin_recv.at[q, g], each_total(q, g))
+
+    def group_scan(q):
+        s, back = q // 2, 1 - q % 2
+        if back:
+            arrived(zin_recv.at[q, pl.ds(0, groups - 1)], slot(Z_IN, q))
+        carry = jnp.zeros((piece, lanes), F32)
+        for n, g in enumerate(range(groups - 1, -1, -1) if back else range(groups)):
+            zout_send[q, g] = carry
+            if not back:
+                carry_out(q, g)
+                if n < groups - 1:
+                    one_total(q, g)
+            if n < groups - 1:
+                carry = decay_z(s, g) * carry + zin_recv[q, g]
+        if back:
+            for g in z_peers:
+                copy(
+                    zout_send.at[q, g], zout_recv.at[q, me_g], Z_OUT, slot(Z_OUT, q), at_group(g)
+                ).start()
+            zout_recv[q, me_g] = zout_send[q, me_g]
 
     def member_scan(q):
-        s, back = q // 2, q % 2
-        other = q - 1 if back else q + 1
+        s, back = q // 2, 1 - q % 2
+        other = q - 1 if q % 2 else q + 1
         arrived(zout_recv.at[q, pl.ds(0, groups - 1)], slot(Z_OUT, q))
         order = range(GROUP - 1, -1, -1) if back else range(GROUP)
         carry = zout_recv[q].reshape(state, lanes)
         carried = [None] * GROUP
         for n, i in enumerate(order):
             carried[i] = carry.astype(BF16)
+            states_out[q, i] = carried[i]
             grad = dot_nt(slices[other, i].astype(BF16), carried[i])
             grad = grad.reshape(ring, cores, part, state)
             for c in range(cores):
@@ -322,8 +347,11 @@
         for c in range(cores):
             grads[q, c, :, me_x] = grads[q, c, :, me_x] + own[:, c]
         copy(grads.at[q, 1 - me_c], pair_recv.at[q], PAIR, slot(PAIR, q), core_other).start()
-        for i in order:
-            cross_send[q, i] = dot(maps[other, i].astype(BF16), carried[i])
+
+    def send_cross(q):
+        other = q - 1 if q % 2 else q + 1
+        for i in range(GROUP):
+            cross_send[q, i] = dot(maps[other, i].astype(BF16), states_out[q, i])
         for x in x_peers:
             copy(
                 cross_send.at[q, x], cross.at[q, me_x], CROSS, slot(CROSS, q), at_x(x)
@@ -341,17 +369,23 @@
         sums_recv[q, me] = sums_send[q, me_r, me_x]
 
     def sum_all(q):
-        s, back = q // 2, q % 2
+        s, back = q // 2, 1 - q % 2
         arrived(sums_recv.at[q, pl.ds(0, len(members))], slot(SUMS, q))
         total = sums_recv[q, 0]
         for n in range(1, ring * GROUP):
             total = total + sums_recv[q, n]
         gbc_ref[1 - back, s] = total
+        written.append(
+            pltpu.make_async_copy(
+                gbc_ref.at[1 - back, s], gbc_out.at[1 - back, s], write_sem.at[streams + q]
+            )
+        )
+        written[-1].start()
 
     written = []
 
     def finish(q):
-        s, back = q // 2, q % 2
+        s, back = q // 2, 1 - q % 2
         arrived(cross.at[q, pl.ds(0, GROUP - 1)], slot(CROSS, q))
         terms = jnp.concatenate([cross[q, j] for j in range(GROUP)], axis=1)
         if back:
@@ -383,7 +417,8 @@
         arrived(dz_recv.at[pl.ds(0, groups - 1)], 1)
 
     work = {
-        "I": send_inputs, "B": pass_maps, "T": group_total, "S": group_scan, "M": member_scan, "C": sum_pair,
+        "I": send_inputs, "B": pass_maps, "T": group_total, "S": group_scan, "M": member_scan, "Y": send_cross,
+        "C": sum_pair,
         "Z": sum_all, "F": finish, "L": local_work,
         "K": lambda n: (hear_near, group_decays, lambda: told(3))[n](), "D": lambda _: all_decays(),
     }
@@ -393,8 +428,8 @@
             work[kind](at)
 
     run(ORDER)
-    last = pltpu.make_async_copy(gbc_ref, gbc_out, write_sem.at[2 * seqs])
-    last.start()
+    for q in range(1, streams, 2):
+        one_total(q, groups - 1)
     sent(dx_send.at[pl.ds(0, GROUP - 1)], 0)
     sent(dz_recv.at[pl.ds(0, groups - 1)], 1)
     sent(maps.at[:, pl.ds(0, GROUP - 1), pl.ds(0, share)], MAPS)
@@ -407,7 +442,6 @@
     sent(sums_recv.at[:, pl.ds(0, len(members))], SUMS)
     for result in written:
         result.wait()
-    last.wait()
 
 
 def write_out(*refs):
@@ -455,16 +489,17 @@
                 pltpu.VMEM((streams, GROUP, rows, state), F32),
                 *[pltpu.VMEM((streams, GROUP, rows, lanes), F32)] * 2,
                 pltpu.VMEM((streams, GROUP, state, lanes), F32),
+                pltpu.VMEM((streams, GROUP, state, lanes), BF16),
                 *[pltpu.VMEM((streams, groups, piece, lanes), F32)] * 4,
                 *[pltpu.VMEM((streams, GROUP, rows, lanes), F32)] * 2,
                 pltpu.VMEM((streams, 2, peers // 2, GROUP, part, state), F32),
                 *[pltpu.VMEM((streams, peers // 2, GROUP, part, state), F32)] * 2,
                 pltpu.VMEM((streams, peers // 2 * GROUP, part, state), F32),
                 pltpu.SemaphoreType.DMA((10,)),
-                pltpu.SemaphoreType.DMA((2 + 8 * streams,)),
+                pltpu.SemaphoreType.DMA((2 + 8 * streams + seqs * groups,)),
                 pltpu.SemaphoreType.DMA((len(args),)),
                 pltpu.SemaphoreType.REGULAR((4,)),
-                pltpu.SemaphoreType.DMA((streams + 1,)),
+                pltpu.SemaphoreType.DMA((2 * streams,)),
             ],
             compiler_params=pltpu.CompilerParams(collective_id=0, has_side_effects=True),
         )(*args)

time: 47 us -> 46.3 us (0.985)
  Pallas kernels: 46.2 us -> 45.5 us
    pallas_call x1, Pallas kernels: 45.5 us -> 44.8 us  [shards(): pl.pallas_call(functools.partial(kernel, (groups, peers)), out_shape=tupl...]
where the time goes in v5:
time: 46.3 us; the launch traced here: 46.2 us
  Pallas kernels  45.5 us (98%)
  between operations  0.64 us (1%)
    pallas_call x1, Pallas kernels, shards(): pl.pallas_call(functools.partial(kernel, (groups, peers)), out_shape=tupl...  44.8 us

profile of v5, /device:TPU:1, one launch (start us, length us, event | category | flops | bytes accessed | tf_op | source)
XLA Modules:
  0.0 46.2 jit_solution(1143261677327282246)
XLA Ops:
  0.6 44.8 %shard_map.85 = (bf16[2,64,512]{2,1,0:T(8,128)(2,1)S(1)}, bf16[2,64,512]{2,1,0:T(8,128)(2,1)S(1)}, f32[2,2,8,128]{3,2,1,0:T(8,128)S(1)}) custom-call(bf16[2,64,512]{2,1,0:T(8,128)(2,1)} %values_in.1, bf16[2,64,128]{2,1,0:T(8,128)(2,1)} %keys_in.1, bf16[2,64,128]{2,1,0:T(8,128)(2,1)} %queries_in.1, f32[2,8,64]{2,1,0:T(8,128)} %forget_in.1, f32[1,8]{1,0:T(1,128)} %bitcast.1, ...), custom_call_target="tpu_custom_call" | custom-call | tf_op jit(solution)/shard_map/pallas_call | solution.py:475
  45.4 0.7 %shard_map.86 = (bf16[2,64,512]{2,1,0:T(8,128)(2,1)}, bf16[2,64,512]{2,1,0:T(8,128)(2,1)}, f32[2,2,8,128]{3,2,1,0:T(8,128)}) custom-call(bf16[2,64,512]{2,1,0:T(8,128)(2,1)S(1)} %get-tuple-element.6.refs_0_, bf16[2,64,512]{2,1,0:T(8,128)(2,1)S(1)} %get-tuple-element.7.refs_1_, f32[2,2,8,128]{3,2,1,0:T(8,128)S(1)} %get-tuple-element.8.refs_2_), custom_call_target="tpu_custom_call" | custom-call | tf_op jit(solution)/shard_map/pallas_call | solution.py:506

commit v6 on v5

--- a/solution.py
+++ b/solution.py
@@ -8,6 +8,7 @@
 from jax.sharding import PartitionSpec as P
 
 MESH = pl.DeviceIdType.MESH
+EARLY = 4
 GROUP = 4
 F32 = jnp.float32
 BF16 = jnp.bfloat16
@@ -31,8 +32,8 @@
 
 ORDER = (
     ("K", 0), ("I", 1), ("B", 0), ("I", 2), ("K", 1), ("T", 0), ("B", 1), ("I", 3), ("L", 0), ("T", 1),
-    ("B", 2), ("L", 1), ("T", 2), ("B", 3), ("D", 0), ("S", 0), ("T", 3), ("S", 1), ("S", 2), ("S", 3),
-    ("K", 2), ("M", 0), ("Y", 0), ("M", 1), ("C", 0), ("Y", 1), ("M", 2), ("C", 1), ("Y", 2), ("C", 2),
+    ("B", 2), ("L", 1), ("T", 2), ("B", 3), ("D", 0), ("S", 0), ("T", 3), ("S", 1), ("S", 2), ("K", 2),
+    ("M", 0), ("S", 3), ("C", 0), ("Y", 0), ("M", 1), ("Y", 1), ("C", 1), ("M", 2), ("Y", 2), ("C", 2),
     ("M", 3), ("C", 3), ("Y", 3), ("F", 0), ("Z", 0), ("F", 1), ("Z", 1), ("Z", 2), ("F", 2), ("F", 3),
     ("Z", 3),
 )
@@ -302,6 +303,11 @@
         def _():
             zout_recv[q, g] = zout_send[q, g]
 
+    def late_out(q, g):
+        copy(
+            zout_send.at[q, g], zout_recv.at[q, me_g], Z_OUT, slot(Z_OUT, q), at_group(g)
+        ).start()
+
     def one_total(q, g):
         @pl.when(me_g != g)
         def _():
@@ -315,7 +321,8 @@
         for n, g in enumerate(range(groups - 1, -1, -1) if back else range(groups)):
             zout_send[q, g] = carry
             if not back:
-                carry_out(q, g)
+                if g < EARLY:
+                    carry_out(q, g)
                 if n < groups - 1:
                     one_total(q, g)
             if n < groups - 1:
@@ -326,6 +333,13 @@
                     zout_send.at[q, g], zout_recv.at[q, me_g], Z_OUT, slot(Z_OUT, q), at_group(g)
                 ).start()
             zout_recv[q, me_g] = zout_send[q, me_g]
+        else:
+            for g in z_peers:
+                pl.when(g >= EARLY)(functools.partial(late_out, q, g))
+
+            @pl.when(me_g >= EARLY)
+            def _():
+                zout_recv[q, me_g] = zout_send[q, me_g]
 
     def member_scan(q):
         s, back = q // 2, 1 - q % 2

time: 46.3 us -> 46.2 us (level)
  no operation moved by 1% of the time
where the time goes in v6:
time: 46.2 us; the launch traced here: 46.1 us
  Pallas kernels  45.4 us (98%)
  between operations  0.64 us (1%)
    pallas_call x1, Pallas kernels, shards(): pl.pallas_call(functools.partial(kernel, (groups, peers)), out_shape=tupl...  44.7 us

profile of v6, /device:TPU:1, one launch (start us, length us, event | category | flops | bytes accessed | tf_op | source)
XLA Modules:
  0.0 46.1 jit_solution(6248624153238119558)
XLA Ops:
  0.6 44.7 %shard_map.85 = (bf16[2,64,512]{2,1,0:T(8,128)(2,1)S(1)}, bf16[2,64,512]{2,1,0:T(8,128)(2,1)S(1)}, f32[2,2,8,128]{3,2,1,0:T(8,128)S(1)}) custom-call(bf16[2,64,512]{2,1,0:T(8,128)(2,1)} %values_in.1, bf16[2,64,128]{2,1,0:T(8,128)(2,1)} %keys_in.1, bf16[2,64,128]{2,1,0:T(8,128)(2,1)} %queries_in.1, f32[2,8,64]{2,1,0:T(8,128)} %forget_in.1, f32[1,8]{1,0:T(1,128)} %bitcast.1, ...), custom_call_target="tpu_custom_call" | custom-call | tf_op jit(solution)/shard_map/pallas_call | solution.py:489
  45.3 0.7 %shard_map.86 = (bf16[2,64,512]{2,1,0:T(8,128)(2,1)}, bf16[2,64,512]{2,1,0:T(8,128)(2,1)}, f32[2,2,8,128]{3,2,1,0:T(8,128)}) custom-call(bf16[2,64,512]{2,1,0:T(8,128)(2,1)S(1)} %get-tuple-element.6.refs_0_, bf16[2,64,512]{2,1,0:T(8,128)(2,1)S(1)} %get-tuple-element.7.refs_1_, f32[2,2,8,128]{3,2,1,0:T(8,128)S(1)} %get-tuple-element.8.refs_2_), custom_call_target="tpu_custom_call" | custom-call | tf_op jit(solution)/shard_map/pallas_call | solution.py:520
